TPU v7x, 32 devices: a whole 2x2x4 slice. The times are simulated.
32 devices in a mesh: groups: 2 (over y), shard: 16 (over z, x, core).
Axes of the slice: x: 2, y: 2, z: 4, core: 2. Of those that a mesh axis runs over, the one named last changes fastest.
Arguments:
- grad_out: bfloat16 [4, 4096, 2048], P('groups', 'shard'), parts along dimension 0, may hold values from -6 to 6
- saved_input: bfloat16 [4, 4096, 2048], P('groups', 'shard'), parts along dimension 0, may hold values from -6 to 6
- lengths: int32 [4], P('groups'), parts along dimension 0, may hold values from 1024 to 4096, as said below
- kernel: float32 [31, 2048], replicated, may hold values from -1 to 1
- gain: float32 [2048], replicated, may hold values from 0.1 to 1.9
- bias: float32 [2048], replicated, may hold values from -4 to 4
- proj_weight: bfloat16 [2048, 2048], P('shard'), may hold values from -0.125 to 0.125
Outputs:
- input_grad: bfloat16 [4, 4096, 2048], P('groups', 'shard'), parts along dimension 0
- proj_grad: float32 [4096, 2048], P(('groups', 'shard')), parts along dimension 0
- kernel_grad: float32 [62, 2048], P('groups', 'shard'), parts along dimension 0
- norm_grads: float32 [4, 2048], P('groups', 'shard'), parts along dimension 0
There are 2 independent parts, one for each index of `groups`. A program takes and returns all parts, laid end to end along the dimension named above; an argument that names none is the same for every part. Nothing has to cross between parts.
Inputs may be any that keep to these rules, and one draw needn't show every extreme that they name: `lengths`: one utterance of every microbatch is live over all 4096 frames.
All inputs are finite; a program needn't handle non-finite values.
Results may differ from a plain program's by a relative error of at most 0.0051.
Values may be sent and summed in bfloat16 or wider, within the bound.
No kernel may reach another device: no remote copies, remote signals or barrier semaphores. Data moves between devices by JAX's collectives and lax.ppermute only.
A program may use at most 128 MiB of HBM per device.

v0:
```python
import functools

import jax
import jax.numpy as jnp
import numpy as np
from jax import lax
from jax.experimental import pallas as pl
from jax.experimental.pallas import tpu as pltpu
from jax.sharding import PartitionSpec as P


LANES = 128
CORES = 2
VMEM_LIMIT = 56 * 1024 * 1024
POINTS = 256


def cost(micros):
    return pl.CostEstimate(flops=0, transcendentals=0, bytes_accessed=int(micros * 3.6e6))


def extended(block, width):
    count = lax.axis_size("shard")
    forward = [(i, i + 1) for i in range(count - 1)]
    backward = [(target, source) for source, target in forward]
    low = lax.ppermute(block[:, block.shape[1] - width :], "shard", forward)
    high = lax.ppermute(block[:, :width], "shard", backward)
    return jnp.concatenate([low, block, high], axis=1)


def frame_mask(lengths, offset, count):
    position = offset + jnp.arange(count, dtype=jnp.int32)
    return (position[None, :] < lengths[:, None])[:, :, None]


def plain_shards(grad_out, saved_input, lengths, kernel, gain, bias, proj_weight):
    batches, frames, model_width = grad_out.shape
    tap_count = kernel.shape[0]
    half_span = (tap_count - 1) // 2
    offset = lax.axis_index("shard") * frames
    norm_scale = lax.rsqrt(jnp.sum(lengths).astype(jnp.float32))
    own_mask = frame_mask(lengths, offset, frames)
    masked_in = jnp.where(own_mask, saved_input, jnp.zeros_like(saved_input))
    masked_grad = jnp.where(own_mask, grad_out, jnp.zeros_like(grad_out))
    in_ext = extended(masked_in, half_span)
    conv = jnp.zeros(grad_out.shape, jnp.float32)
    for tap in range(tap_count):
        conv = conv + kernel[tap] * in_ext[:, tap : tap + frames].astype(jnp.float32)
    pre_act = gain * conv + bias
    gate_sig = jax.nn.sigmoid(pre_act)
    activated = (pre_act * gate_sig).astype(jnp.bfloat16)
    rows = masked_grad.reshape(batches * frames, model_width)
    weight = lax.all_gather(proj_weight, "shard", axis=0, tiled=True)
    act_grad = lax.dot_general(
        rows, weight, (((1,), (1,)), ((), ())), preferred_element_type=jnp.float32
    ).reshape(batches, frames, model_width)
    pre_grad = act_grad * gate_sig * (1.0 + pre_act * (1.0 - gate_sig))
    conv_grad = (pre_grad * gain).astype(jnp.bfloat16)
    grad_ext = extended(conv_grad, half_span)
    back_sum = jnp.zeros(grad_out.shape, jnp.float32)
    grad_float = conv_grad.astype(jnp.float32)
    tap_rows = []
    for tap in range(tap_count):
        begin = 2 * half_span - tap
        back_sum = back_sum + kernel[tap] * grad_ext[:, begin : begin + frames].astype(jnp.float32)
        tap_rows.append(
            jnp.sum(in_ext[:, tap : tap + frames].astype(jnp.float32) * grad_float, axis=(0, 1))
        )
    input_grad = jnp.where(own_mask, back_sum, 0.0).astype(jnp.bfloat16)
    tap_rows.append(jnp.sum(pre_grad * conv, axis=(0, 1)))
    tap_rows.append(jnp.sum(pre_grad, axis=(0, 1)))
    stats = jnp.stack(tap_rows, 0) * norm_scale
    summed = lax.psum_scatter(stats, "shard", scatter_dimension=1, tiled=True)
    product = lax.dot_general(
        activated.reshape(batches * frames, model_width),
        rows,
        (((0,), (0,)), ((), ())),
        preferred_element_type=jnp.float32,
    )
    proj_grad = lax.psum_scatter(product * norm_scale, "shard", scatter_dimension=0, tiled=True)
    return (input_grad, proj_grad, summed[:tap_count], summed[tap_count:])


class Plan:
    def __init__(self, count, groups, batches, frames, model_width, tap_count):
        self.count = count
        self.chips = count // CORES
        self.rounds = self.chips // 2
        self.batches = batches
        self.frames = frames
        self.chip_frames = CORES * frames
        self.width = model_width
        self.block = model_width // count
        self.taps = tap_count
        self.half = (tap_count - 1) // 2
        self.ghalo = -(-self.half // 16) * 16
        self.xhalo = 2 * self.ghalo
        self.ext = self.chip_frames + 2 * self.ghalo
        self.xext = self.chip_frames + 2 * self.xhalo
        self.tap_rows = -(-tap_count // 16) * 16
        self.stat_rows = self.tap_rows + 8
        self.weight_parts = 2 if groups == 2 else 1
        self.pairs = [(h, 1 - h) for h in range(self.rounds, 0, -1)]
        self.conv_windows = windows(self.ext, self.xhalo - self.ghalo - self.half + tap_count)
        self.back_windows = windows(self.chip_frames, self.ghalo + self.half + 1)

    def window_rows(self, found):
        return found[0] * (found[1] - 1) + POINTS

    def block_slot(self, step, side):
        return 3 + self.batches + 2 * step + side

    def usable(self):
        return (
            self.count % (2 * CORES) == 0
            and self.block == LANES
            and self.block * self.count == self.width
            and self.frames % 128 == 0
            and self.frames >= self.xhalo
            and self.taps % 2 == 1
            and 4 * self.ghalo <= POINTS // 2
            and self.window_rows(self.conv_windows) >= self.xext
            and self.window_rows(self.back_windows) >= self.ext
            and self.window_rows(self.conv_windows)
            >= self.xhalo + self.window_rows(self.back_windows) - self.back_windows[0]
            and self.chips == 8
            and self.batches == 2
        )

    def chip_at(self, position):
        half = self.chips // 2
        return jnp.where(position < half, 2 * position, 2 * (self.chips - 1 - position) + 1)

    def position_of(self, chip):
        return jnp.where(chip % 2 == 0, chip // 2, self.chips - 1 - chip // 2)

    def ring(self):
        half = self.chips // 2
        order = [2 * i for i in range(half)] + [2 * i + 1 for i in reversed(range(half))]
        forward = []
        for core in range(CORES):
            for i in range(self.chips):
                source, target = order[i], order[(i + 1) % self.chips]
                forward.append((CORES * source + core, CORES * target + core))
        return forward, [(t, s) for s, t in forward]

    def edges(self):
        pairs = []
        for chip in range(self.chips - 1):
            last, first = CORES * chip + 1, CORES * (chip + 1)
            pairs += [(last, first), (first, last)]
        return pairs

    def edges_like(self):
        pairs = []
        for chip in range(self.chips - 1):
            pairs.append((CORES * chip + 1, CORES * (chip + 1) + 1))
            pairs.append((CORES * (chip + 1), CORES * chip))
        return pairs

    def partners(self):
        return [(s, s ^ 1) for s in range(self.count)]


def sigmoid(value):
    return 0.5 * jnp.tanh(0.5 * value) + 0.5


def split(value):
    high = value.astype(jnp.bfloat16)
    return high, (value - high.astype(jnp.float32)).astype(jnp.bfloat16)


def split_matrix(matrix):
    high = matrix.astype(jnp.bfloat16)
    return high, (matrix - high.astype(np.float64)).astype(jnp.bfloat16)


def transforms(plan):
    time = np.arange(POINTS)
    theta = np.pi * (2 * np.arange(POINTS // 2) + 1) / POINTS
    angle = theta[:, None] * time[None, :]
    direct = np.concatenate([np.cos(angle), -np.sin(angle)], 0)
    inverse = direct.T * (2.0 / POINTS)

    def spectrum(lags):
        phase = theta[:, None] * lags[None, :]
        matrix = np.concatenate([np.cos(phase), np.sin(phase)], 0)
        return np.pad(matrix, ((0, 0), (0, plan.tap_rows - plan.taps)))

    taps = np.arange(plan.taps)
    back_lags = plan.ghalo + plan.half - taps
    lag_rows = np.pad(inverse[back_lags], ((0, plan.tap_rows - plan.taps), (0, 0)))
    half = lambda m: m.astype(jnp.bfloat16)
    conv_lags = plan.xhalo - plan.ghalo - plan.half + taps
    return (
        half(direct),
        half(inverse),
        np.stack(split_matrix(spectrum(conv_lags))),
        np.stack(split_matrix(spectrum(back_lags))),
        np.stack(split_matrix(lag_rows)),
        half(direct * (time < plan.back_windows[0])),
    )


def taps_spectrum(t_ref, k_ref):
    high, low = split(jnp.concatenate([k_ref[0][...], k_ref[1][...]], axis=1))
    dot = functools.partial(jnp.dot, preferred_element_type=jnp.float32)
    return dot(t_ref[0], high) + dot(t_ref[1], high) + dot(t_ref[0], low)


def to_spectrum(direct_ref, window):
    return jnp.dot(direct_ref[...], window, preferred_element_type=jnp.float32)


def from_spectrum(inverse_ref, rows, parts, slot):
    return jnp.dot(inverse_ref[:rows, :], parts[slot], preferred_element_type=jnp.float32)


def windows(rows_out, reach):
    count = -(-rows_out // ((POINTS - reach) // 16 * 16))
    return -(-rows_out // count // 16) * 16, count


STEP = 16
HALF = POINTS // 2


def spectral_product(spec, taps, parts, slot):
    for row in range(0, HALF, STEP):
        up, down = slice(row, row + STEP), slice(HALF + row, HALF + row + STEP)
        re, im, kr, ks = spec[slot, up, :], spec[slot, down, :], taps[up, :], taps[down, :]
        parts[slot, up, :] = (re * kr - im * ks).astype(jnp.bfloat16)
        parts[slot, down, :] = (re * ks + im * kr).astype(jnp.bfloat16)


def conv_body(plan, info, *refs):
    own_x, other_x, near_x, far_x, k_ref, gain_ref, bias_ref = (
        refs[2 * i : 2 * i + 2] for i in range(7)
    )
    direct, inverse, t_ref, own_g, other_g = refs[14:19]
    conv_ref, x_ref, out_f, out_b, spec, taps, parts, act, acc = refs[19:]
    each, count = plan.conv_windows
    f, xh, gh, cf = plan.frames, plan.xhalo, plan.ghalo, plan.chip_frames
    b = pl.program_id(0)
    core, offset, live = info[0], info[1], info[3 + b]

    @pl.when(b == 0)
    def _():
        taps[...] = taps_spectrum(t_ref, k_ref)

    def put(row, pair):
        for part in range(0, pair[0].shape[1], STEP):
            position = lax.broadcasted_iota(jnp.int32, (STEP, LANES), 0) + (
                offset - xh + row + part
            )
            keep = jnp.where(position < live, 1.0, 0.0).astype(jnp.bfloat16)
            for side in range(2):
                lanes = slice(side * LANES, (side + 1) * LANES)
                x_ref[0, row + part : row + part + STEP, lanes] = (
                    pair[side][0, part : part + STEP, :] * keep
                )

    @pl.when(core == 0)
    def _():
        put(0, near_x)
        put(xh, own_x)
        put(xh + f, other_x)
        put(xh + 2 * f, far_x)

    @pl.when(core != 0)
    def _():
        put(0, far_x)
        put(xh, other_x)
        put(xh + f, own_x)
        put(xh + 2 * f, near_x)

    x_ref[0, plan.xext :, :] = jnp.zeros((x_ref.shape[1] - plan.xext, 2 * LANES), jnp.bfloat16)

    for j in range(count):
        spec[j] = to_spectrum(direct, x_ref[0, j * each : j * each + POINTS, :])
    for j in range(count):
        spectral_product(spec, taps, parts, j)
        rows = min(each, plan.ext - j * each)
        conv_ref[0, j * each : j * each + rows, :] = from_spectrum(inverse, rows, parts, j)

    for i in range(cf // LANES):
        for side in range(2):
            lanes = slice(side * LANES, (side + 1) * LANES)
            begin = gh + i * LANES
            conv = conv_ref[0, begin : begin + LANES, lanes]
            pre = gain_ref[side][...] * conv + bias_ref[side][...]
            position = lax.broadcasted_iota(jnp.int32, (LANES, LANES), 0) + (offset + i * LANES)
            value = jnp.where(position < live, pre * sigmoid(pre), 0.0)
            act[lanes, i * LANES : (i + 1) * LANES] = value.T.astype(jnp.bfloat16)

    own = pl.multiple_of(core * f, f)
    other = pl.multiple_of((1 - core) * f, f)

    def product(columns):
        dot = functools.partial(jnp.dot, preferred_element_type=jnp.float32)
        return dot(act[:, pl.ds(own, f)], own_g[0, :, columns]) + dot(
            act[:, pl.ds(other, f)], other_g[0, :, columns]
        )

    tiles = [slice(c, c + 2 * LANES) for c in range(0, plan.width, 2 * LANES)]

    @pl.when(b == 0)
    def _():
        for columns in tiles:
            acc[:, columns] = product(columns)

    @pl.when(b != 0)
    def _():
        for columns in tiles:
            total = acc[:, columns] + product(columns)
            if plan.batches > 2:
                acc[:, columns] = total
            out_f[:, columns] = total[:LANES].astype(out_f.dtype)
            out_b[:, columns] = total[LANES:].astype(out_b.dtype)


def pair_specs(plan, step, shape, index):
    return [
        pl.BlockSpec(
            shape, lambda b, info, at=plan.block_slot(step, side): index(b, info[at])
        )
        for side in range(2)
    ]


def whole(array):
    return pl.BlockSpec(
        array.shape, lambda *_: (0,) * array.ndim, pipeline_mode=pl.Buffered(1)
    )


def conv_call(plan, step, info, x, xp, xa, xb, g, gp, kernel, gain, bias, consts, kind):
    bt = plan.batches
    flat = lambda b, block: (0, block)
    fixed = lambda b, info: (0, 0)
    direct, inverse, t_conv = consts[:3]
    wide = 2 * LANES
    slots = plan.conv_windows[1]
    specs = functools.partial(pair_specs, plan, step)
    frames, halo = (1, plan.frames, LANES), (1, plan.xhalo, LANES)
    by_batch = lambda b, block: (b, 0, block)
    by_chip = lambda b, block: (b, 0, block // CORES)
    x_rows = plan.window_rows(plan.conv_windows)
    return pl.pallas_call(
        functools.partial(conv_body, plan),
        grid_spec=pltpu.PrefetchScalarGridSpec(
            num_scalar_prefetch=1,
            grid=(bt,),
            in_specs=specs(frames, by_batch)
            + specs(frames, by_batch)
            + specs(halo, by_chip)
            + specs(halo, by_chip)
            + specs((plan.tap_rows, LANES), flat)
            + specs((1, LANES), flat)
            + specs((1, LANES), flat)
            + [whole(direct), whole(inverse), whole(t_conv)]
            + [pl.BlockSpec((1, plan.frames, plan.width), lambda b, info: (b, 0, 0))] * 2,
            out_specs=[
                pl.BlockSpec((1, plan.ext, wide), lambda b, info: (b, 0, 0)),
                pl.BlockSpec((1, x_rows, wide), lambda b, info: (b, 0, 0)),
                pl.BlockSpec((LANES, plan.width), fixed),
                pl.BlockSpec((LANES, plan.width), fixed),
            ],
            scratch_shapes=[
                pltpu.VMEM((slots, POINTS, wide), jnp.float32),
                pltpu.VMEM((POINTS, wide), jnp.float32),
                pltpu.VMEM((slots, POINTS, wide), jnp.bfloat16),
                pltpu.VMEM((wide, plan.chip_frames), jnp.bfloat16),
                pltpu.VMEM((wide, plan.width), jnp.float32),
            ],
        ),
        out_shape=[
            jax.ShapeDtypeStruct((bt, plan.ext, wide), jnp.float32),
            jax.ShapeDtypeStruct((bt, x_rows, wide), jnp.bfloat16),
            jax.ShapeDtypeStruct((LANES, plan.width), kind),
            jax.ShapeDtypeStruct((LANES, plan.width), kind),
        ],
        compiler_params=pltpu.CompilerParams(vmem_limit_bytes=VMEM_LIMIT),
        cost_estimate=cost(6.0),
        name="conv",
    )(info, x, x, xp, xp, xa, xa, xb, xb, kernel, kernel, gain, gain, bias, bias,
      direct, inverse, t_conv, g, gp)


def back_body(plan, steps, earlier, sources, info, *refs):
    pairs = len(steps)
    g_refs = refs[:4]
    k_refs, gain_refs, bias_refs = (
        refs[4 + 2 * pairs * i : 4 + 2 * pairs * (i + 1)] for i in range(3)
    )
    refs = refs[4 + 6 * pairs :]
    conv_refs, x_refs, w_refs = refs[:pairs], refs[pairs : 2 * pairs], refs[2 * pairs : -28]
    (own_ref, send_ref, stat_ref, weight, mg, conv_buf, x_buf, ag_first, ag_second, gs, tail,
     spec, xspec, taps, cross, parts, os, flat, w_sem, c_sem, x_sem, g_sem) = refs[-22:]
    direct, segment, inverse, t_ref, lag_ref, before_ref = refs[-28:-22]
    core, offset, side_y = info[0], info[1], info[2]
    f, xh, gh, cf, ext = plan.frames, plan.xhalo, plan.ghalo, plan.chip_frames, plan.ext
    each, count = plan.back_windows
    turn = pl.program_id(0)

    def weight_copies(pair):
        made = []
        for n, (array, part, target, begin, rows) in enumerate(sources[pair]):
            first, into = begin, target * LANES
            if part is not None:
                into = pl.multiple_of(target * LANES + (side_y + part) % 2 * rows, rows)
            made.append(
                pltpu.make_async_copy(
                    w_refs[array].at[pl.ds(first, rows), :],
                    weight.at[pair, pl.ds(into, rows), :],
                    w_sem.at[pair, n],
                )
            )
        return made

    def frame_copies(pair):
        return [
            pltpu.make_async_copy(conv_refs[pair].at[i], conv_buf.at[pair, i], c_sem.at[pair, i])
            for i in range(plan.batches)
        ] + [
            pltpu.make_async_copy(x_refs[pair].at[i], x_buf.at[pair, i], x_sem.at[pair, i])
            for i in range(plan.batches)
        ]

    def grad_copies(b):
        own, other, near, far = g_refs
        moves = []
        for ref, turned in ((own, core), (other, 1 - core)):
            moves.append((ref.at[b], pl.multiple_of(gh + turned * f, gh), f, 0, plan.width))
        width = plan.width // CORES
        for ref, turned in ((near, core), (far, 1 - core)):
            for part in range(CORES):
                piece = ref.at[b, pl.ds(xh + part * gh, gh), :]
                moves.append((piece, pl.multiple_of(turned * (gh + cf), gh), gh, part * width, width))
        return [
            pltpu.make_async_copy(
                source, mg.at[b, pl.ds(row, rows), pl.ds(column, columns)], g_sem.at[b, n]
            )
            for n, (source, row, rows, column, columns) in enumerate(moves)
        ]

    def act_grad(pair, b):
        return lax.dot_general(
            mg[b], weight[pair], (((1,), (1,)), ((), ())), preferred_element_type=jnp.float32
        )

    @pl.when(turn == 0)
    def _():
        for copy in weight_copies(0) + grad_copies(0) + frame_copies(0) + grad_copies(1):
            copy.start()
        for pair in range(1, pairs):
            for copy in weight_copies(pair) + frame_copies(pair):
                copy.start()
        for b in range(plan.batches):
            gs[b, ext:, :] = jnp.zeros((gs.shape[1] - ext, 2 * LANES), jnp.bfloat16)
            tail[b] = jnp.zeros(tail.shape[1:], tail.dtype)
        for copy in weight_copies(0) + grad_copies(0):
            copy.wait()
        ag_first[...] = act_grad(0, 0)
        for copy in frame_copies(0) + grad_copies(1):
            copy.wait()

    for pair in range(pairs):

        @pl.when(turn == pair)
        def _():
            taps[...] = taps_spectrum(t_ref, k_refs[2 * pair : 2 * pair + 2])
            for row, pick in ((0, gain_refs), (8, bias_refs)):
                for side in range(2):
                    lanes = slice(side * LANES, (side + 1) * LANES)
                    flat[row : row + 8, lanes] = jnp.broadcast_to(
                        pick[2 * pair + side][...], (8, LANES)
                    )
            if pair > 0:
                for copy in frame_copies(pair):
                    copy.wait()
            if pair + 1 < pairs:
                for copy in weight_copies(pair + 1):
                    copy.wait()

    gain, bias = flat[:1, :], flat[8:9, :]
    last_rows = cf - (count - 1) * each
    fold = lambda v: jnp.sum(v.reshape(STEP // 8, 8, 2 * LANES), axis=0)
    gain_sum = jnp.zeros((8, 2 * LANES), jnp.float32)
    bias_sum = jnp.zeros((8, 2 * LANES), jnp.float32)
    for b in range(plan.batches):
        live = info[3 + b]
        here, ahead = (ag_first, ag_second) if b == 0 else (ag_second, ag_first)
        following = turn if b == 0 else jnp.minimum(turn + 1, pairs - 1)
        ahead[...] = act_grad(following, 1 - b)
        for j in range(count):
            begin = xh + j * each
            if j < count - 1:
                window = x_buf[turn, b, begin : begin + POINTS, :]
            else:
                tail[b, :last_rows, :] = x_buf[turn, b, begin : begin + last_rows, :]
                window = tail[b]
            xspec[b * count + j] = to_spectrum(segment, window)
        for row in range(0, ext, STEP):
            conv = conv_buf[turn, b, row : row + STEP, :]
            pre = gain * conv + bias
            sig = sigmoid(pre)
            value = here[row : row + STEP, :] * sig * (1.0 + pre * (1.0 - sig))
            position = lax.broadcasted_iota(jnp.int32, value.shape, 0) + (offset - gh + row)
            value = jnp.where(position < live, value, 0.0)
            gs[b, row : row + STEP, :] = (value * gain).astype(jnp.bfloat16)
            if gh <= row < gh + cf:
                gain_sum = gain_sum + fold(value * conv)
                bias_sum = bias_sum + fold(value)
        for j in range(count):
            spec[b * count + j] = to_spectrum(direct, gs[b, j * each : j * each + POINTS, :])
        for j in range(count):
            slot = b * count + j
            spectral_product(spec, taps, parts, slot)
            rows = min(each, cf - j * each)
            value = from_spectrum(inverse, rows, parts, slot)
            position = offset + j * each + lax.broadcasted_iota(jnp.int32, value.shape, 0)
            os[b, j * each : j * each + rows, :] = jnp.where(
                position < live, value, 0.0
            ).astype(jnp.bfloat16)

    for row in range(0, HALF, STEP):
        up, down = slice(row, row + STEP), slice(HALF + row, HALF + row + STEP)
        total_r = total_i = jnp.zeros((STEP, 2 * LANES), jnp.float32)
        for j in range(plan.batches * count):
            re, im, xr, xi = spec[j, up, :], spec[j, down, :], xspec[j, up, :], xspec[j, down, :]
            total_r = total_r + (re * xr + im * xi)
            total_i = total_i + (im * xr - re * xi)
        cross[up, :] = total_r
        cross[down, :] = total_i

    @pl.when(core == 0)
    def _():
        own_ref[0] = os[:, :f]
        send_ref[0] = os[:, f:]

    @pl.when(core != 0)
    def _():
        own_ref[0] = os[:, f:]
        send_ref[0] = os[:, :f]

    high, low = split(cross[...])
    dot = functools.partial(jnp.dot, preferred_element_type=jnp.float32)
    taps_total = dot(lag_ref[0], high) + dot(lag_ref[1], high) + dot(lag_ref[0], low)
    total = [jnp.sum(value, axis=0, keepdims=True) for value in (gain_sum, bias_sum)]
    pad = jnp.zeros((plan.stat_rows - plan.tap_rows - 2, 2 * LANES), jnp.float32)
    total = jnp.concatenate([taps_total] + total + [pad], axis=0)
    if earlier is None:
        stat_ref[0] = total
        return
    for side in range(2):
        lanes = slice(side * LANES, (side + 1) * LANES)
        chip = info[plan.block_slot(steps[0], side) - 2 * turn] // CORES
        stat_ref[chip] = total[:, lanes]
        for n, step in enumerate(earlier):
            chip = info[plan.block_slot(step, side)] // CORES
            stat_ref[chip] = before_ref[n, :, lanes]


def back_call(
    plan, steps, info, grads, sources, arrays, convs, xs, kernel, gain, bias, consts, before, earlier
):
    bt, pairs = plan.batches, len(steps)
    direct, inverse, _, t_back, lags, segment = consts
    wide = 2 * LANES
    slots = bt * plan.back_windows[1]
    any_space = pl.BlockSpec(memory_space=pl.ANY)

    def by_block(shape):
        return [
            pl.BlockSpec(
                shape, lambda p, info, at=plan.block_slot(step, side): (0, info[at]),
                pipeline_mode=pl.Buffered(1),
            )
            for step in steps for side in range(2)
        ]

    frames = (bt, plan.frames, wide)
    each = pl.BlockSpec((1,) + frames, lambda p, info: (p, 0, 0, 0))
    most = max(len(source) for source in sources)
    stat_shape = (pairs, plan.stat_rows, wide)
    stat_spec = pl.BlockSpec((1, plan.stat_rows, wide), lambda p, info: (p, 0, 0))
    if before is None:
        earlier, before = None, jnp.zeros((8, LANES), jnp.float32)
    else:
        stat_shape = (plan.chips, plan.stat_rows, LANES)
        stat_spec = pl.BlockSpec(stat_shape, lambda p, info: (0, 0, 0))
    return pl.pallas_call(
        functools.partial(back_body, plan, steps, earlier, sources),
        grid_spec=pltpu.PrefetchScalarGridSpec(
            num_scalar_prefetch=1,
            grid=(pairs,),
            in_specs=[any_space] * len(grads)
            + by_block((plan.tap_rows, LANES))
            + by_block((1, LANES))
            + by_block((1, LANES))
            + [any_space] * (2 * pairs + len(arrays))
            + [whole(c) for c in (direct, segment, inverse, t_back, lags, before)],
            out_specs=[
                each,
                each,
                stat_spec,
            ],
            scratch_shapes=[
                pltpu.VMEM((pairs, wide, plan.width), jnp.bfloat16),
                pltpu.VMEM((bt, plan.ext, plan.width), jnp.bfloat16),
                pltpu.VMEM((pairs, bt, plan.ext, wide), jnp.float32),
                pltpu.VMEM((pairs, bt, xs[0].shape[1], wide), jnp.bfloat16),
                pltpu.VMEM((plan.ext, wide), jnp.float32),
                pltpu.VMEM((plan.ext, wide), jnp.float32),
                pltpu.VMEM((bt, plan.window_rows(plan.back_windows), wide), jnp.bfloat16),
                pltpu.VMEM((bt, POINTS, wide), jnp.bfloat16),
                pltpu.VMEM((slots, POINTS, wide), jnp.float32),
                pltpu.VMEM((slots, POINTS, wide), jnp.float32),
                pltpu.VMEM((POINTS, wide), jnp.float32),
                pltpu.VMEM((POINTS, wide), jnp.float32),
                pltpu.VMEM((slots, POINTS, wide), jnp.bfloat16),
                pltpu.VMEM((bt, plan.chip_frames, wide), jnp.bfloat16),
                pltpu.VMEM((16, wide), jnp.float32),
                pltpu.SemaphoreType.DMA((pairs, most)),
                pltpu.SemaphoreType.DMA((pairs, bt)),
                pltpu.SemaphoreType.DMA((pairs, bt)),
                pltpu.SemaphoreType.DMA((bt, 2 + 2 * CORES)),
            ],
        ),
        out_shape=[
            jax.ShapeDtypeStruct((pairs,) + frames, jnp.bfloat16),
            jax.ShapeDtypeStruct((pairs,) + frames, jnp.bfloat16),
            jax.ShapeDtypeStruct(stat_shape, jnp.float32),
        ],
        compiler_params=pltpu.CompilerParams(vmem_limit_bytes=VMEM_LIMIT),
        cost_estimate=cost(6.0 * pairs),
        name="back",
    )(info, *grads, *[kernel] * 2 * pairs, *[gain] * 2 * pairs, *[bias] * 2 * pairs,
      *convs, *xs, *arrays, direct, segment, inverse, t_back, lags, before)


def place_body(plan, calls, info, *refs):
    out_ref = refs[-1]
    for i, ref in enumerate(refs[:-1]):
        for turn, step in enumerate(calls[i // 2]):
            for side in range(2):
                block = info[plan.block_slot(step, side)]
                if i % 2:
                    block = block + 1 - 2 * info[0]
                column = pl.multiple_of(block * LANES, LANES)
                lanes = slice(side * LANES, (side + 1) * LANES)
                out_ref[:, :, pl.ds(column, LANES)] = ref[turn, :, :, lanes]


def place_call(plan, calls, info, arrays):
    shape = (plan.batches, plan.frames, plan.width)
    return pl.pallas_call(
        functools.partial(place_body, plan, calls),
        grid_spec=pltpu.PrefetchScalarGridSpec(
            num_scalar_prefetch=1,
            grid=(1,),
            in_specs=[whole(array) for array in arrays],
            out_specs=pl.BlockSpec(shape, lambda g, info: (0, 0, 0)),
        ),
        out_shape=jax.ShapeDtypeStruct(shape, jnp.bfloat16),
        compiler_params=pltpu.CompilerParams(vmem_limit_bytes=VMEM_LIMIT),
        cost_estimate=cost(3.0),
        name="place",
    )(info, *arrays)


def edge_body(plan, x_first, x_last, g_first, g_last, near_ref, far_ref):
    core = lax.axis_index("shard") % CORES

    def take(owner, x_ref, grad_ref):
        for i in range(plan.chips):
            for out, parity in ((near_ref, 1 - owner), (far_ref, owner)):
                column = (CORES * i + parity) * LANES
                out[:, : plan.xhalo, i * LANES : (i + 1) * LANES] = x_ref[
                    :, :, column : column + LANES
                ]
        for part in range(CORES):
            row = plan.xhalo + part * plan.ghalo
            width = plan.width // CORES
            near_ref[:, row : row + plan.ghalo, :] = grad_ref[
                :, :, part * width : (part + 1) * width
            ]

    pl.when(core == 0)(lambda: take(0, x_first, g_first))
    pl.when(core != 0)(lambda: take(1, x_last, g_last))


def edge_call(plan, x, g):
    def spec(rows, first):
        shape = (plan.batches, rows, plan.width)
        block = 0 if first else plan.frames // rows - 1
        return pl.BlockSpec(shape, lambda i: (0, block, 0))

    xh, gh = plan.xhalo, plan.ghalo
    shapes = [
        (plan.batches, rows, plan.width // CORES) for rows in (xh + CORES * gh, xh)
    ]
    return pl.pallas_call(
        functools.partial(edge_body, plan),
        grid=(1,),
        in_specs=[spec(xh, True), spec(xh, False), spec(gh, True), spec(gh, False)],
        out_specs=[pl.BlockSpec(shape, lambda i: (0, 0, 0)) for shape in shapes],
        out_shape=[jax.ShapeDtypeStruct(shape, jnp.bfloat16) for shape in shapes],
        cost_estimate=cost(1.0),
        name="edge",
    )(x, x, g, g)


def after(value, *others):
    return lax.optimization_barrier((value, *others))[0]


def ring_shards(plan, grad_out, saved_input, lengths, kernel, gain, bias, proj_weight):
    index = lax.axis_index("shard")
    group = lax.axis_index("groups")
    core, chip = index % CORES, index // CORES
    place = plan.position_of(chip)
    forward, backward = plan.ring()
    offset = chip * plan.chip_frames
    scale = lax.rsqrt(jnp.sum(lengths).astype(jnp.float32))
    pairs = plan.pairs
    far = jnp.asarray([d for pair in pairs for d in pair], jnp.int32)
    owned = CORES * plan.chip_at((place + far + plan.chips) % plan.chips) + core
    info = jnp.concatenate([jnp.stack([core, offset, group]), lengths, owned]).astype(jnp.int32)
    gain2, bias2 = gain.reshape(1, -1), bias.reshape(1, -1)
    taps = jnp.pad(kernel, ((0, plan.tap_rows - plan.taps), (0, 0)))
    consts = [jnp.asarray(c) for c in transforms(plan)]

    x_near, x_far = edge_call(plan, saved_input, grad_out)
    xa = lax.ppermute(x_near, "shard", plan.edges())
    xb = lax.ppermute(x_far, "shard", plan.edges_like())
    xp = lax.ppermute(saved_input, "shard", plan.partners())
    mgp = lax.ppermute(grad_out, "shard", plan.partners())

    halved = plan.weight_parts == 2
    piece = LANES // 2
    around = {}
    going = [proj_weight] * 2
    if halved:
        going = [lax.dynamic_slice_in_dim(proj_weight, group * piece, piece, 0)] * 2
    xa, xb, taps, info, scale = lax.optimization_barrier((xa, xb, taps, info, scale))

    def weight_round(step):
        going[0] = lax.ppermute(going[0], "shard", forward)
        around[-step] = going[0]
        if step < plan.rounds:
            going[1] = lax.ppermute(going[1], "shard", backward)
            around[step] = going[1]
        else:
            around[step] = around.pop(-step)

    convs, xs, products = [], [], []

    def conv_step(step, order):
        conv, x, *product = conv_call(
            plan, step, order, saved_input, xp, xa, xb, grad_out,
            mgp, taps, gain2, bias2, consts, jnp.bfloat16 if step == 0 else jnp.float32,
        )
        convs.append(conv)
        xs.append(x)
        products.append(product)

    def sum_round(step, send, *behind):
        received = (
            lax.ppermute(send[0], "shard", forward), lax.ppermute(send[1], "shard", backward)
        )
        kinds = (jnp.bfloat16, jnp.bfloat16 if step < plan.rounds - 1 else jnp.float32)
        own = lax.optimization_barrier((*products[step], *received, *behind))[:2]
        return [
            (product + value.astype(jnp.float32)).astype(kind)
            for product, value, kind in zip(own, received, kinds)
        ]

    def wait_for(value):
        going[:] = lax.optimization_barrier((*going, value))[:2]

    weight_round(1)
    conv_step(0, info)
    xc = lax.ppermute(after(xa, products[0][0]), "shard", plan.partners())
    wait_for(products[0][0])
    weight_round(2)
    conv_step(1, after(info, products[0][0]))
    wait_for(products[1][0])
    weight_round(3)
    conv_step(2, after(info, products[1][0]))
    wait_for(products[2][0])
    weight_round(4)
    send = sum_round(1, products[0], products[2][0])
    conv_step(3, after(info, products[2][0], *send))
    send = sum_round(2, send, products[3][0])

    arrays = [proj_weight]
    source = {0: [(0, None, 0, LANES)]}

    def keep(array):
        arrays.append(array)
        return len(arrays) - 1

    swap = [
        (g * plan.count + s, (1 - g) * plan.count + s) for g in range(2) for s in range(plan.count)
    ]
    for distances in ([1, -1], [2, -2], [3, -3, 4]):
        if not halved:
            for d in distances:
                source[d] = [(keep(around[d]), None, 0, LANES)]
            continue
        swapped = keep(
            lax.ppermute(
                jnp.concatenate([around[d] for d in distances], 0),
                ("groups", "shard"), swap,
            )
        )
        for i, d in enumerate(distances):
            source[d] = [(keep(around[d]), 0, 0, piece), (swapped, 1, i * piece, piece)]

    calls = [(3, 2), (1, 0)]
    pieces, stats = [], None
    for steps in calls:
        if steps == calls[-1]:
            send = sum_round(3, send, pieces[0])
        order = after(info, products[-1][0], *send)
        used = sorted({a[0] for step in steps for d in pairs[step] for a in source[d]})
        sources = [
            [
                (used.index(array), part, block, begin, rows)
                for block, d in enumerate(pairs[step])
                for array, part, begin, rows in source[d]
            ]
            for step in steps
        ]
        own, given, stat = back_call(
            plan, steps, order, (grad_out, mgp, xa, xc), sources, [arrays[i] for i in used],
            [convs[step] for step in steps], [xs[step] for step in steps],
            taps, gain2, bias2, consts, stats, calls[0],
        )
        stats = stat
        pieces += [own, lax.ppermute(given, "shard", plan.partners())]
    recv_f = after(lax.ppermute(send[0], "shard", forward), stats)
    proj_grad = (send[1] + recv_f.astype(jnp.float32)) * scale
    groups = [[CORES * p + c for p in range(plan.chips)] for c in range(CORES)]
    shares = lax.all_to_all(stats, "shard", 0, 0, axis_index_groups=groups)
    full = place_call(plan, calls, after(info, stats), pieces)
    summed = jnp.sum(after(shares, full, proj_grad), axis=0) * scale
    return (
        full, proj_grad, summed[: plan.taps], summed[plan.tap_rows : plan.tap_rows + 2]
    )


def shards(count, group_count, grad_out, saved_input, lengths, kernel, gain, bias, proj_weight):
    batches, frames, model_width = grad_out.shape
    plan = Plan(count, group_count, batches, frames, model_width, kernel.shape[0])
    args = (grad_out, saved_input, lengths, kernel, gain, bias, proj_weight)
    return ring_shards(plan, *args) if plan.usable() else plain_shards(*args)


def solution(mesh):
    placed = (
        P("groups", "shard", None),
        P("groups", "shard", None),
        P("groups"),
        P(),
        P(),
        P(),
        P("shard", None),
    )

    def body(*args):
        return shards(mesh.shape["shard"], mesh.shape["groups"], *args)

    return jax.shard_map(
        body,
        mesh=mesh,
        in_specs=placed,
        out_specs=(
            P("groups", "shard", None),
            P(("groups", "shard"), None),
            P("groups", "shard"),
            P("groups", "shard"),
        ),
        check_vma=False,
    )
```

profile of v0, /device:TPU:0, one launch (start us, length us, event | category | flops | bytes accessed | tf_op | source)
XLA Modules:
  0.0 137.5 jit_solution(7901534251446157435)
XLA Ops:
  1.3 1.9 %edge.1 = (bf16[2,64,1024]{2,1,0:T(8,128)(2,1)}, bf16[2,32,1024]{2,1,0:T(8,128)(2,1)}) custom-call(bf16[2,256,2048]{2,1,0:T(8,128)(2,1)} %refs_1_.7, bf16[2,256,2048]{2,1,0:T(8,128)(2,1)} %refs_1_.7, bf16[2,256,2048]{2,1,0:T(8,128)(2,1)} %refs_0_.11, bf16[2,256,2048]{2,1,0:T(8,128)(2,1)} %refs_0_.11), custom_call_target="tpu_custom_call" | custom-call | bytes 3600000 | tf_op jit(solution)/shard_map/edge/pallas_call | solution.py:705
  8.0 6.0 %collective-permute-done.1.refs_6_.refs_7_ = bf16[2,32,1024]{2,1,0:T(8,128)(2,1)S(1)} collective-permute-done((bf16[2,32,1024]{2,1,0:T(8,128)(2,1)}, bf16[2,32,1024]{2,1,0:T(8,128)(2,1)S(1)}, u32[]{:S(2)}, u32[]{:S(2)}) %collective-permute-start.1) | collective-permute-done | bytes 131104 | tf_op jit(solution)/shard_map/ppermute | solution.py:738
  15.4 7.3 %conv.4 = (f32[2,544,256]{2,1,0:T(8,128)}, bf16[2,640,256]{2,1,0:T(8,128)(2,1)}, bf16[128,2048]{1,0:T(8,128)(2,1)}, bf16[128,2048]{1,0:T(8,128)(2,1)}) custom-call(s32[13]{0:T(128)} %concatenate.12.info, bf16[2,256,2048]{2,1,0:T(8,128)(2,1)} %refs_1_.7, bf16[2,256,2048]{2,1,0:T(8,128)(2,1)} %refs_1_.7, bf16[2,256,2048]{2,1,0:T(8,128)(2,1)} %copy-done, ...), custom_call_target="tpu_custom_call" | custom-call | bytes 21600000 | tf_op jit(solution)/shard_map/conv/pallas_call | solution.py:350
  22.8 6.1 %collective-permute-start.4 = (bf16[128,2048]{1,0:T(8,128)(2,1)}, bf16[128,2048]{1,0:T(8,128)(2,1)S(1)}, u32[]{:S(2)}, u32[]{:S(2)}) collective-permute-start(bf16[128,2048]{1,0:T(8,128)(2,1)} %get-tuple-element.59), channel_id=1, source_target_pairs={{0,4},{4,8},{8,12},{12,14},{14,10},{10,6},{6,2},{2,0},{1,5},{5,9},... | collective-permute-start | bytes 1572872 | tf_op jit(solution)/shard_map/ppermute | solution.py:772
  28.8 2.1 %collective-permute-start.12 = (bf16[64,2048]{1,0:T(8,128)(2,1)S(1)}, bf16[64,2048]{1,0:T(8,128)(2,1)S(1)}, u32[]{:S(2)}, u32[]{:S(2)}) collective-permute-start(bf16[64,2048]{1,0:T(8,128)(2,1)S(1)} %constant_dynamic-slice_fusion), channel_id=1, source_target_pairs={{0,4},{4,8},{8,12},{12,14},{14,10},{10,6},{6,2},{2,0},{1,5},{5,9},... | collective-permute-start | bytes 786440 | tf_op jit(solution)/shard_map/ppermute | solution.py:751
  30.9 7.6 %conv.5 = (f32[2,544,256]{2,1,0:T(8,128)}, bf16[2,640,256]{2,1,0:T(8,128)(2,1)}, f32[128,2048]{1,0:T(8,128)}, f32[128,2048]{1,0:T(8,128)}) custom-call(s32[13]{0:T(128)} %concatenate.12.info, bf16[2,256,2048]{2,1,0:T(8,128)(2,1)} %refs_1_.7, bf16[2,256,2048]{2,1,0:T(8,128)(2,1)} %refs_1_.7, bf16[2,256,2048]{2,1,0:T(8,128)(2,1)} %copy-done, ...), custom_call_target="tpu_custom_call" | custom-call | bytes 21600000 | tf_op jit(solution)/shard_map/conv/pallas_call | solution.py:350
  38.5 6.5 %collective-permute-done.12.refs_23_ = bf16[64,2048]{1,0:T(8,128)(2,1)S(1)} collective-permute-done((bf16[64,2048]{1,0:T(8,128)(2,1)S(1)}, bf16[64,2048]{1,0:T(8,128)(2,1)S(1)}, u32[]{:S(2)}, u32[]{:S(2)}) %collective-permute-start.12) | collective-permute-done | bytes 262176 | tf_op jit(solution)/shard_map/ppermute | solution.py:751
  45.1 2.1 %collective-permute-done.11.refs_22_ = bf16[64,2048]{1,0:T(8,128)(2,1)S(1)} collective-permute-done((bf16[64,2048]{1,0:T(8,128)(2,1)S(1)}, bf16[64,2048]{1,0:T(8,128)(2,1)S(1)}, u32[]{:S(2)}, u32[]{:S(2)}) %collective-permute-start.11) | collective-permute-done | bytes 262176 | tf_op jit(solution)/shard_map/ppermute | solution.py:754
  47.2 1.6 %collective-permute-start.15 = (bf16[64,2048]{1,0:T(8,128)(2,1)S(1)}, bf16[64,2048]{1,0:T(8,128)(2,1)S(1)}, u32[]{:S(2)}, u32[]{:S(2)}) collective-permute-start(bf16[64,2048]{1,0:T(8,128)(2,1)S(1)} %collective-permute-done.12.refs_23_), channel_id=1, source_target_pairs={{0,4},{4,8},{8,12},{12,14},{14,10},{10,6},{6,2},{2,0},{1,5},{5,9},... | collective-permute-start | bytes 786440 | tf_op jit(solution)/shard_map/ppermute | solution.py:751
  49.2 7.6 %conv.6 = (f32[2,544,256]{2,1,0:T(8,128)}, bf16[2,640,256]{2,1,0:T(8,128)(2,1)}, f32[128,2048]{1,0:T(8,128)}, f32[128,2048]{1,0:T(8,128)}) custom-call(s32[13]{0:T(128)} %concatenate.12.info, bf16[2,256,2048]{2,1,0:T(8,128)(2,1)} %refs_1_.7, bf16[2,256,2048]{2,1,0:T(8,128)(2,1)} %refs_1_.7, bf16[2,256,2048]{2,1,0:T(8,128)(2,1)} %copy-done, ...), custom_call_target="tpu_custom_call" | custom-call | bytes 21600000 | tf_op jit(solution)/shard_map/conv/pallas_call | solution.py:350
  57.0 1.6 %collective-permute-start.6 = (bf16[128,2048]{1,0:T(8,128)(2,1)S(1)}, bf16[128,2048]{1,0:T(8,128)(2,1)S(1)}, u32[]{:S(2)}, u32[]{:S(2)}) collective-permute-start(bf16[128,2048]{1,0:T(8,128)(2,1)S(1)} %add_convert_fusion.4), channel_id=1, source_target_pairs={{0,4},{4,8},{8,12},{12,14},{14,10},{10,6},{6,2},{2,0},{1,5},{5,9},... | collective-permute-start | bytes 1572872 | tf_op jit(solution)/shard_map/ppermute | solution.py:772
  59.3 1.6 %collective-permute-start.18 = (bf16[64,2048]{1,0:T(8,128)(2,1)S(1)}, bf16[64,2048]{1,0:T(8,128)(2,1)S(1)}, u32[]{:S(2)}, u32[]{:S(2)}) collective-permute-start(bf16[64,2048]{1,0:T(8,128)(2,1)S(1)} %collective-permute-done.15.refs_21_), channel_id=1, source_target_pairs={{0,4},{4,8},{8,12},{12,14},{14,10},{10,6},{6,2},{2,0},{1,5},{5,9},... | collective-permute-start | bytes 786440 | tf_op jit(solution)/shard_map/ppermute | solution.py:751
  61.4 1.6 %collective-permute-start.13 = (bf16[128,2048]{1,0:T(8,128)(2,1)S(1)}, bf16[128,2048]{1,0:T(8,128)(2,1)S(1)}, u32[]{:S(2)}, u32[]{:S(2)}) collective-permute-start(bf16[128,2048]{1,0:T(8,128)(2,1)S(1)} %pad_maximum_fusion.1), channel_id=1, source_target_pairs={{0,16},{1,17},{2,18},{3,19},{4,20},{5,21},{6,22},{7,23},{8,24},{9,... | collective-permute-start | bytes 1572872 | tf_op jit(solution)/shard_map/ppermute | solution.py:815
  63.0 12.0 %collective-permute-done.18.refs_24_ = bf16[64,2048]{1,0:T(8,128)(2,1)S(1)} collective-permute-done((bf16[64,2048]{1,0:T(8,128)(2,1)S(1)}, bf16[64,2048]{1,0:T(8,128)(2,1)S(1)}, u32[]{:S(2)}, u32[]{:S(2)}) %collective-permute-start.18) | collective-permute-done | bytes 262176 | tf_op jit(solution)/shard_map/ppermute | solution.py:751
  78.1 7.6 %conv.7 = (f32[2,544,256]{2,1,0:T(8,128)}, bf16[2,640,256]{2,1,0:T(8,128)(2,1)}, f32[128,2048]{1,0:T(8,128)}, f32[128,2048]{1,0:T(8,128)}) custom-call(s32[13]{0:T(128)} %concatenate.12.info, bf16[2,256,2048]{2,1,0:T(8,128)(2,1)} %refs_1_.7, bf16[2,256,2048]{2,1,0:T(8,128)(2,1)} %refs_1_.7, bf16[2,256,2048]{2,1,0:T(8,128)(2,1)} %copy-done, ...), custom_call_target="tpu_custom_call" | custom-call | bytes 21600000 | tf_op jit(solution)/shard_map/conv/pallas_call | solution.py:350
  85.9 1.8 %collective-permute-start.8 = (bf16[128,2048]{1,0:T(8,128)(2,1)S(1)}, bf16[128,2048]{1,0:T(8,128)(2,1)S(1)}, u32[]{:S(2)}, u32[]{:S(2)}) collective-permute-start(bf16[128,2048]{1,0:T(8,128)(2,1)S(1)} %add_convert_fusion.2), channel_id=1, source_target_pairs={{0,4},{4,8},{8,12},{12,14},{14,10},{10,6},{6,2},{2,0},{1,5},{5,9},... | collective-permute-start | bytes 1572872 | tf_op jit(solution)/shard_map/ppermute | solution.py:772
  89.0 1.6 %collective-permute-start.20 = (bf16[192,2048]{1,0:T(8,128)(2,1)S(1)}, bf16[192,2048]{1,0:T(8,128)(2,1)S(1)}, u32[]{:S(2)}, u32[]{:S(2)}) collective-permute-start(bf16[192,2048]{1,0:T(8,128)(2,1)S(1)} %pad_maximum_fusion), channel_id=1, source_target_pairs={{0,16},{1,17},{2,18},{3,19},{4,20},{5,21},{6,22},{7,23},{8,24},{9,... | collective-permute-start | bytes 2359304 | tf_op jit(solution)/shard_map/ppermute | solution.py:815
  91.6 12.3 %back.2 = (bf16[2,2,256,256]{3,2,1,0:T(8,128)(2,1)}, bf16[2,2,256,256]{3,2,1,0:T(8,128)(2,1)}, f32[2,40,256]{2,1,0:T(8,128)}) custom-call(s32[13]{0:T(128)} %concatenate.12.info, bf16[2,256,2048]{2,1,0:T(8,128)(2,1)} %refs_0_.11, bf16[2,256,2048]{2,1,0:T(8,128)(2,1)} %collective-permute-done.3.refs_18_.refs_1_, bf16[2,64,1024]{2,1,0:T(8,128)(2,1)} %copy-done.1, ...), custom_call_target="tpu_custom_call" | custom-call | bytes 43200000 | tf_op jit(solution)/shard_map/back/pallas_call | solution.py:594
  104.4 1.8 %collective-permute-start.23 = (bf16[128,2048]{1,0:T(8,128)(2,1)S(1)}, bf16[128,2048]{1,0:T(8,128)(2,1)S(1)}, u32[]{:S(2)}, u32[]{:S(2)}) collective-permute-start(bf16[128,2048]{1,0:T(8,128)(2,1)S(1)} %add_convert_fusion), channel_id=1, source_target_pairs={{0,4},{4,8},{8,12},{12,14},{14,10},{10,6},{6,2},{2,0},{1,5},{5,9},... | collective-permute-start | bytes 1572872 | tf_op jit(solution)/shard_map/ppermute | solution.py:845
  106.3 2.7 %collective-permute-done.20.refs_22_ = bf16[192,2048]{1,0:T(8,128)(2,1)S(1)} collective-permute-done((bf16[192,2048]{1,0:T(8,128)(2,1)S(1)}, bf16[192,2048]{1,0:T(8,128)(2,1)S(1)}, u32[]{:S(2)}, u32[]{:S(2)}) %collective-permute-start.20) | collective-permute-done | bytes 786464 | tf_op jit(solution)/shard_map/ppermute | solution.py:815
  109.9 12.5 %back.3 = (bf16[2,2,256,256]{3,2,1,0:T(8,128)(2,1)}, bf16[2,2,256,256]{3,2,1,0:T(8,128)(2,1)}, f32[8,40,128]{2,1,0:T(8,128)}) custom-call(s32[13]{0:T(128)} %concatenate.12.info, bf16[2,256,2048]{2,1,0:T(8,128)(2,1)} %refs_0_.11, bf16[2,256,2048]{2,1,0:T(8,128)(2,1)} %collective-permute-done.3.refs_18_.refs_1_, bf16[2,64,1024]{2,1,0:T(8,128)(2,1)} %copy-done.1, ...), custom_call_target="tpu_custom_call" | custom-call | bytes 43200000 | tf_op jit(solution)/shard_map/back/pallas_call | solution.py:594
  122.5 5.7 %all-to-all-start = ((f32[8,40,128]{2,1,0:T(8,128)}), f32[8,40,128]{2,1,0:T(8,128)S(1)}, u32[]{:S(2)}, u32[]{:S(2)}) async-start(f32[8,40,128]{2,1,0:T(8,128)} %get-tuple-element.94), calls=%async_computation | async-start | bytes 327680 | tf_op jit(solution)/shard_map/all_to_all | solution.py:848
  129.2 4.1 %place.1 = bf16[2,256,2048]{2,1,0:T(8,128)(2,1)} custom-call(s32[13]{0:T(128)} %concatenate.12.info, bf16[2,2,256,256]{3,2,1,0:T(8,128)(2,1)} %get-tuple-element.82.refs_0_, bf16[2,2,256,256]{3,2,1,0:T(8,128)(2,1)} %copy-done.22, bf16[2,2,256,256]{3,2,1,0:T(8,128)(2,1)} %get-tuple-element.97.refs_2_, bf16[2,2,256,256]{3,2,1,0:T(8,128)(2,1)} %copy-done.23), custom_call_target="tpu_custom_call" | custom-call | bytes 10800000 | tf_op jit(solution)/shard_map/place/pallas_call | solution.py:659
  134.5 1.9 %all-to-all-done = f32[8,40,128]{2,1,0:T(8,128)S(1)} async-done(((f32[8,40,128]{2,1,0:T(8,128)}), f32[8,40,128]{2,1,0:T(8,128)S(1)}, u32[]{:S(2)}, u32[]{:S(2)}) %all-to-all-start) | async-done | bytes 163872 | tf_op jit(solution)/shard_map/all_to_all | solution.py:848
  (108 shorter events, 18.0 us)
Async XLA Ops:
  0.7 13.3 %collective-permute-start.2 = (bf16[2,256,2048]{2,1,0:T(8,128)(2,1)}, bf16[2,256,2048]{2,1,0:T(8,128)(2,1)S(1)}, u32[]{:S(2)}, u32[]{:S(2)}) collective-permute-start(bf16[2,256,2048]{2,1,0:T(8,128)(2,1)} %refs_1_.7), channel_id=1, source_target_pairs={{0,1},{1,0},{2,3},{3,2},{4,5},{5,4},{6,7},{7,6},{8,9},{9,8},{10,11... | collective-permute-start | bytes 6291464 | tf_op jit(solution)/shard_map/ppermute | solution.py:739
  1.2 12.8 %collective-permute-start.3 = (bf16[2,256,2048]{2,1,0:T(8,128)(2,1)}, bf16[2,256,2048]{2,1,0:T(8,128)(2,1)}, u32[]{:S(2)}, u32[]{:S(2)}) collective-permute-start(bf16[2,256,2048]{2,1,0:T(8,128)(2,1)} %refs_0_.11), channel_id=1, source_target_pairs={{0,1},{1,0},{2,3},{3,2},{4,5},{5,4},{6,7},{7,6},{8,9},{9,8},{10,11... | collective-permute-start | bytes 6291464 | tf_op jit(solution)/shard_map/ppermute | solution.py:740
  3.2 10.8 %collective-permute-start = (bf16[2,64,1024]{2,1,0:T(8,128)(2,1)}, bf16[2,64,1024]{2,1,0:T(8,128)(2,1)S(1)}, u32[]{:S(2)}, u32[]{:S(2)}) collective-permute-start(bf16[2,64,1024]{2,1,0:T(8,128)(2,1)} %get-tuple-element.53), channel_id=1, source_target_pairs={{1,2},{2,1},{3,4},{4,3},{5,6},{6,5},{7,8},{8,7},{9,10},{10,9},{11,... | collective-permute-start | bytes 786440 | tf_op jit(solution)/shard_map/ppermute | solution.py:737
  3.9 10.1 %collective-permute-start.1 = (bf16[2,32,1024]{2,1,0:T(8,128)(2,1)}, bf16[2,32,1024]{2,1,0:T(8,128)(2,1)S(1)}, u32[]{:S(2)}, u32[]{:S(2)}) collective-permute-start(bf16[2,32,1024]{2,1,0:T(8,128)(2,1)} %get-tuple-element.54), channel_id=1, source_target_pairs={{1,3},{2,0},{3,5},{4,2},{5,7},{6,4},{7,9},{8,6},{9,11},{10,8},{11,... | collective-permute-start | bytes 393224 | tf_op jit(solution)/shard_map/ppermute | solution.py:738
  22.8 34.1 %collective-permute-start.4 = (bf16[128,2048]{1,0:T(8,128)(2,1)}, bf16[128,2048]{1,0:T(8,128)(2,1)S(1)}, u32[]{:S(2)}, u32[]{:S(2)}) collective-permute-start(bf16[128,2048]{1,0:T(8,128)(2,1)} %get-tuple-element.59), channel_id=1, source_target_pairs={{0,4},{4,8},{8,12},{12,14},{14,10},{10,6},{6,2},{2,0},{1,5},{5,9},... | collective-permute-start | bytes 1572872 | tf_op jit(solution)/shard_map/ppermute | solution.py:772
  28.8 28.0 %collective-permute-start.5 = (bf16[128,2048]{1,0:T(8,128)(2,1)}, bf16[128,2048]{1,0:T(8,128)(2,1)S(1)}, u32[]{:S(2)}, u32[]{:S(2)}) collective-permute-start(bf16[128,2048]{1,0:T(8,128)(2,1)} %get-tuple-element.65), channel_id=1, source_target_pairs={{4,0},{8,4},{12,8},{14,12},{10,14},{6,10},{2,6},{0,2},{5,1},{9,5},... | collective-permute-start | bytes 1572872 | tf_op jit(solution)/shard_map/ppermute | solution.py:772
  28.8 16.2 %collective-permute-start.12 = (bf16[64,2048]{1,0:T(8,128)(2,1)S(1)}, bf16[64,2048]{1,0:T(8,128)(2,1)S(1)}, u32[]{:S(2)}, u32[]{:S(2)}) collective-permute-start(bf16[64,2048]{1,0:T(8,128)(2,1)S(1)} %constant_dynamic-slice_fusion), channel_id=1, source_target_pairs={{0,4},{4,8},{8,12},{12,14},{14,10},{10,6},{6,2},{2,0},{1,5},{5,9},... | collective-permute-start | bytes 786440 | tf_op jit(solution)/shard_map/ppermute | solution.py:751
  30.9 16.3 %collective-permute-start.11 = (bf16[64,2048]{1,0:T(8,128)(2,1)S(1)}, bf16[64,2048]{1,0:T(8,128)(2,1)S(1)}, u32[]{:S(2)}, u32[]{:S(2)}) collective-permute-start(bf16[64,2048]{1,0:T(8,128)(2,1)S(1)} %constant_dynamic-slice_fusion), channel_id=1, source_target_pairs={{4,0},{8,4},{12,8},{14,12},{10,14},{6,10},{2,6},{0,2},{5,1},{9,5},... | collective-permute-start | bytes 786440 | tf_op jit(solution)/shard_map/ppermute | solution.py:754
  47.2 12.0 %collective-permute-start.15 = (bf16[64,2048]{1,0:T(8,128)(2,1)S(1)}, bf16[64,2048]{1,0:T(8,128)(2,1)S(1)}, u32[]{:S(2)}, u32[]{:S(2)}) collective-permute-start(bf16[64,2048]{1,0:T(8,128)(2,1)S(1)} %collective-permute-done.12.refs_23_), channel_id=1, source_target_pairs={{0,4},{4,8},{8,12},{12,14},{14,10},{10,6},{6,2},{2,0},{1,5},{5,9},... | collective-permute-start | bytes 786440 | tf_op jit(solution)/shard_map/ppermute | solution.py:751
  48.8 10.5 %collective-permute-start.14 = (bf16[64,2048]{1,0:T(8,128)(2,1)S(1)}, bf16[64,2048]{1,0:T(8,128)(2,1)S(1)}, u32[]{:S(2)}, u32[]{:S(2)}) collective-permute-start(bf16[64,2048]{1,0:T(8,128)(2,1)S(1)} %collective-permute-done.11.refs_22_), channel_id=1, source_target_pairs={{4,0},{8,4},{12,8},{14,12},{10,14},{6,10},{2,6},{0,2},{5,1},{9,5},... | collective-permute-start | bytes 786440 | tf_op jit(solution)/shard_map/ppermute | solution.py:754
  57.0 28.7 %collective-permute-start.6 = (bf16[128,2048]{1,0:T(8,128)(2,1)S(1)}, bf16[128,2048]{1,0:T(8,128)(2,1)S(1)}, u32[]{:S(2)}, u32[]{:S(2)}) collective-permute-start(bf16[128,2048]{1,0:T(8,128)(2,1)S(1)} %add_convert_fusion.4), channel_id=1, source_target_pairs={{0,4},{4,8},{8,12},{12,14},{14,10},{10,6},{6,2},{2,0},{1,5},{5,9},... | collective-permute-start | bytes 1572872 | tf_op jit(solution)/shard_map/ppermute | solution.py:772
  58.7 27.0 %collective-permute-start.7 = (bf16[128,2048]{1,0:T(8,128)(2,1)S(1)}, bf16[128,2048]{1,0:T(8,128)(2,1)S(1)}, u32[]{:S(2)}, u32[]{:S(2)}) collective-permute-start(bf16[128,2048]{1,0:T(8,128)(2,1)S(1)} %add_convert_fusion.3), channel_id=1, source_target_pairs={{4,0},{8,4},{12,8},{14,12},{10,14},{6,10},{2,6},{0,2},{5,1},{9,5},... | collective-permute-start | bytes 1572872 | tf_op jit(solution)/shard_map/ppermute | solution.py:772
  59.3 15.8 %collective-permute-start.18 = (bf16[64,2048]{1,0:T(8,128)(2,1)S(1)}, bf16[64,2048]{1,0:T(8,128)(2,1)S(1)}, u32[]{:S(2)}, u32[]{:S(2)}) collective-permute-start(bf16[64,2048]{1,0:T(8,128)(2,1)S(1)} %collective-permute-done.15.refs_21_), channel_id=1, source_target_pairs={{0,4},{4,8},{8,12},{12,14},{14,10},{10,6},{6,2},{2,0},{1,5},{5,9},... | collective-permute-start | bytes 786440 | tf_op jit(solution)/shard_map/ppermute | solution.py:751
  60.9 15.7 %collective-permute-start.17 = (bf16[64,2048]{1,0:T(8,128)(2,1)S(1)}, bf16[64,2048]{1,0:T(8,128)(2,1)S(1)}, u32[]{:S(2)}, u32[]{:S(2)}) collective-permute-start(bf16[64,2048]{1,0:T(8,128)(2,1)S(1)} %collective-permute-done.14.refs_25_), channel_id=1, source_target_pairs={{4,0},{8,4},{12,8},{14,12},{10,14},{6,10},{2,6},{0,2},{5,1},{9,5},... | collective-permute-start | bytes 786440 | tf_op jit(solution)/shard_map/ppermute | solution.py:754
  61.4 27.6 %collective-permute-start.13 = (bf16[128,2048]{1,0:T(8,128)(2,1)S(1)}, bf16[128,2048]{1,0:T(8,128)(2,1)S(1)}, u32[]{:S(2)}, u32[]{:S(2)}) collective-permute-start(bf16[128,2048]{1,0:T(8,128)(2,1)S(1)} %pad_maximum_fusion.1), channel_id=1, source_target_pairs={{0,16},{1,17},{2,18},{3,19},{4,20},{5,21},{6,22},{7,23},{8,24},{9,... | collective-permute-start | bytes 1572872 | tf_op jit(solution)/shard_map/ppermute | solution.py:815
  75.0 15.6 %collective-permute-start.16 = (bf16[128,2048]{1,0:T(8,128)(2,1)S(1)}, bf16[128,2048]{1,0:T(8,128)(2,1)S(1)}, u32[]{:S(2)}, u32[]{:S(2)}) collective-permute-start(bf16[128,2048]{1,0:T(8,128)(2,1)S(1)} %pad_maximum_fusion.2), channel_id=1, source_target_pairs={{0,16},{1,17},{2,18},{3,19},{4,20},{5,21},{6,22},{7,23},{8,24},{9,... | collective-permute-start | bytes 1572872 | tf_op jit(solution)/shard_map/ppermute | solution.py:815
  76.6 12.3 %collective-permute-start.19 = (bf16[64,2048]{1,0:T(8,128)(2,1)S(1)}, bf16[64,2048]{1,0:T(8,128)(2,1)S(1)}, u32[]{:S(2)}, u32[]{:S(2)}) collective-permute-start(bf16[64,2048]{1,0:T(8,128)(2,1)S(1)} %collective-permute-done.18.refs_24_), channel_id=1, source_target_pairs={{0,4},{4,8},{8,12},{12,14},{14,10},{10,6},{6,2},{2,0},{1,5},{5,9},... | collective-permute-start | bytes 786440 | tf_op jit(solution)/shard_map/ppermute | solution.py:751
  85.9 18.4 %collective-permute-start.8 = (bf16[128,2048]{1,0:T(8,128)(2,1)S(1)}, bf16[128,2048]{1,0:T(8,128)(2,1)S(1)}, u32[]{:S(2)}, u32[]{:S(2)}) collective-permute-start(bf16[128,2048]{1,0:T(8,128)(2,1)S(1)} %add_convert_fusion.2), channel_id=1, source_target_pairs={{0,4},{4,8},{8,12},{12,14},{14,10},{10,6},{6,2},{2,0},{1,5},{5,9},... | collective-permute-start | bytes 1572872 | tf_op jit(solution)/shard_map/ppermute | solution.py:772
  88.5 15.7 %collective-permute-start.9 = (bf16[128,2048]{1,0:T(8,128)(2,1)}, bf16[128,2048]{1,0:T(8,128)(2,1)S(1)}, u32[]{:S(2)}, u32[]{:S(2)}) collective-permute-start(bf16[128,2048]{1,0:T(8,128)(2,1)} %add_convert_fusion.1), channel_id=1, source_target_pairs={{4,0},{8,4},{12,8},{14,12},{10,14},{6,10},{2,6},{0,2},{5,1},{9,5},... | collective-permute-start | bytes 1572872 | tf_op jit(solution)/shard_map/ppermute | solution.py:772
  89.0 20.0 %collective-permute-start.20 = (bf16[192,2048]{1,0:T(8,128)(2,1)S(1)}, bf16[192,2048]{1,0:T(8,128)(2,1)S(1)}, u32[]{:S(2)}, u32[]{:S(2)}) collective-permute-start(bf16[192,2048]{1,0:T(8,128)(2,1)S(1)} %pad_maximum_fusion), channel_id=1, source_target_pairs={{0,16},{1,17},{2,18},{3,19},{4,20},{5,21},{6,22},{7,23},{8,24},{9,... | collective-permute-start | bytes 2359304 | tf_op jit(solution)/shard_map/ppermute | solution.py:815
  103.9 24.3 %collective-permute-start.21 = (bf16[2,2,256,256]{3,2,1,0:T(8,128)(2,1)}, bf16[2,2,256,256]{3,2,1,0:T(8,128)(2,1)S(1)}, u32[]{:S(2)}, u32[]{:S(2)}) collective-permute-start(bf16[2,2,256,256]{3,2,1,0:T(8,128)(2,1)} %get-tuple-element.96), channel_id=1, source_target_pairs={{0,1},{1,0},{2,3},{3,2},{4,5},{5,4},{6,7},{7,6},{8,9},{9,8},{10,11... | collective-permute-start | bytes 1572872 | tf_op jit(solution)/shard_map/ppermute | solution.py:844
  104.4 23.8 %collective-permute-start.23 = (bf16[128,2048]{1,0:T(8,128)(2,1)S(1)}, bf16[128,2048]{1,0:T(8,128)(2,1)S(1)}, u32[]{:S(2)}, u32[]{:S(2)}) collective-permute-start(bf16[128,2048]{1,0:T(8,128)(2,1)S(1)} %add_convert_fusion), channel_id=1, source_target_pairs={{0,4},{4,8},{8,12},{12,14},{14,10},{10,6},{6,2},{2,0},{1,5},{5,9},... | collective-permute-start | bytes 1572872 | tf_op jit(solution)/shard_map/ppermute | solution.py:845
  122.4 5.8 %collective-permute-start.22 = (bf16[2,2,256,256]{3,2,1,0:T(8,128)(2,1)}, bf16[2,2,256,256]{3,2,1,0:T(8,128)(2,1)S(1)}, u32[]{:S(2)}, u32[]{:S(2)}) collective-permute-start(bf16[2,2,256,256]{3,2,1,0:T(8,128)(2,1)} %get-tuple-element.98), channel_id=1, source_target_pairs={{0,1},{1,0},{2,3},{3,2},{4,5},{5,4},{6,7},{7,6},{8,9},{9,8},{10,11... | collective-permute-start | bytes 1572872 | tf_op jit(solution)/shard_map/ppermute | solution.py:844
  122.5 13.8 %all-to-all-start = ((f32[8,40,128]{2,1,0:T(8,128)}), f32[8,40,128]{2,1,0:T(8,128)S(1)}, u32[]{:S(2)}, u32[]{:S(2)}) async-start(f32[8,40,128]{2,1,0:T(8,128)} %get-tuple-element.94), calls=%async_computation | async-start | bytes 327680 | tf_op jit(solution)/shard_map/all_to_all | solution.py:848
  (28 other events, 229.1 us)
where the time goes:
time: 138 us
  Pallas kernels  61 us (44%)
  starting transfers between devices  33.2 us (24%)
  waiting for transfers between devices  31.3 us (23%)
  local copies, waits for them, and re-layouts  6.83 us (5%)
  other arithmetic  3.34 us (2%)
  between operations  1.82 us (1%)
    pallas_call x4, Pallas kernels, conv_call(): pl.pallas_call(functools.partial(conv_body, plan), grid_spec=pltpu.Prefet...  30.2 us
    pallas_call x2, Pallas kernels, back_call(): pl.pallas_call(functools.partial(back_body, plan, steps, earlier, sources...  24.8 us
    ppermute x4, waiting for transfers between devices, weight_round(): going[0] = lax.ppermute(going[0], 'shard', forward)  18.5 us
    ppermute x3, starting transfers between devices, sum_round(): lax.ppermute(send[0], 'shard', forward)  9.47 us
    ppermute x4, starting transfers between devices, weight_round(): going[0] = lax.ppermute(going[0], 'shard', forward)  6.76 us
    ppermute x1, waiting for transfers between devices, ring_shards(): xb = lax.ppermute(x_far, 'shard', plan.edges_like())  6.02 us
    all_to_all x1, starting transfers between devices, ring_shards(): shares = lax.all_to_all(stats, 'shard', 0, 0, axis_index_groups=groups)  5.73 us
    ppermute x3, starting transfers between devices, ring_shards(): lax.ppermute(jnp.concatenate([around[d] for d in distances], 0), ('groups...  4.69 us
  transfers between devices with their start and end apart: 25, of which 6 were waited for; matrix products, arithmetic and copies ran while one was open for 4% of the time, Pallas kernels for 39%

commit v1 on v0

--- a/solution.py
+++ b/solution.py
@@ -239,27 +239,34 @@
         refs[2 * i : 2 * i + 2] for i in range(7)
     )
     direct, inverse, t_ref, own_g, other_g = refs[14:19]
-    conv_ref, x_ref, out_f, out_b, spec, taps, parts, act, acc = refs[19:]
+    conv_ref, x_ref, out_f, out_b, spec, taps, parts, act, acc, grad, sem = refs[19:]
     each, count = plan.conv_windows
     f, xh, gh, cf = plan.frames, plan.xhalo, plan.ghalo, plan.chip_frames
-    b = pl.program_id(0)
-    core, offset, live = info[0], info[1], info[3 + b]
-
-    @pl.when(b == 0)
-    def _():
-        taps[...] = taps_spectrum(t_ref, k_ref)
+    core, offset = info[0], info[1]
+
+    copies = [
+        pltpu.make_async_copy(
+            ref.at[b], grad.at[b, pl.ds(pl.multiple_of(turned * f, f), f), :], sem.at[b, n]
+        )
+        for b in range(plan.batches)
+        for n, (ref, turned) in enumerate(((own_g, core), (other_g, 1 - core)))
+    ]
+    for copy in copies:
+        copy.start()
+    taps[...] = taps_spectrum(t_ref, k_ref)
 
     def put(row, pair):
-        for part in range(0, pair[0].shape[1], STEP):
-            position = lax.broadcasted_iota(jnp.int32, (STEP, LANES), 0) + (
-                offset - xh + row + part
-            )
-            keep = jnp.where(position < live, 1.0, 0.0).astype(jnp.bfloat16)
-            for side in range(2):
-                lanes = slice(side * LANES, (side + 1) * LANES)
-                x_ref[0, row + part : row + part + STEP, lanes] = (
-                    pair[side][0, part : part + STEP, :] * keep
+        for b in range(plan.batches):
+            for part in range(0, pair[0].shape[1], STEP):
+                position = lax.broadcasted_iota(jnp.int32, (STEP, LANES), 0) + (
+                    offset - xh + row + part
                 )
+                keep = jnp.where(position < info[3 + b], 1.0, 0.0).astype(jnp.bfloat16)
+                for side in range(2):
+                    lanes = slice(side * LANES, (side + 1) * LANES)
+                    x_ref[b, row + part : row + part + STEP, lanes] = (
+                        pair[side][b, part : part + STEP, :] * keep
+                    )
 
     @pl.when(core == 0)
     def _():
@@ -275,49 +282,47 @@
         put(xh + f, own_x)
         put(xh + 2 * f, near_x)
 
-    x_ref[0, plan.xext :, :] = jnp.zeros((x_ref.shape[1] - plan.xext, 2 * LANES), jnp.bfloat16)
-
-    for j in range(count):
-        spec[j] = to_spectrum(direct, x_ref[0, j * each : j * each + POINTS, :])
-    for j in range(count):
-        spectral_product(spec, taps, parts, j)
-        rows = min(each, plan.ext - j * each)
-        conv_ref[0, j * each : j * each + rows, :] = from_spectrum(inverse, rows, parts, j)
-
-    for i in range(cf // LANES):
-        for side in range(2):
-            lanes = slice(side * LANES, (side + 1) * LANES)
-            begin = gh + i * LANES
-            conv = conv_ref[0, begin : begin + LANES, lanes]
-            pre = gain_ref[side][...] * conv + bias_ref[side][...]
-            position = lax.broadcasted_iota(jnp.int32, (LANES, LANES), 0) + (offset + i * LANES)
-            value = jnp.where(position < live, pre * sigmoid(pre), 0.0)
-            act[lanes, i * LANES : (i + 1) * LANES] = value.T.astype(jnp.bfloat16)
-
-    own = pl.multiple_of(core * f, f)
-    other = pl.multiple_of((1 - core) * f, f)
-
-    def product(columns):
-        dot = functools.partial(jnp.dot, preferred_element_type=jnp.float32)
-        return dot(act[:, pl.ds(own, f)], own_g[0, :, columns]) + dot(
-            act[:, pl.ds(other, f)], other_g[0, :, columns]
-        )
-
+    x_ref[:, plan.xext :, :] = jnp.zeros(
+        (plan.batches, x_ref.shape[1] - plan.xext, 2 * LANES), jnp.bfloat16
+    )
     tiles = [slice(c, c + 2 * LANES) for c in range(0, plan.width, 2 * LANES)]
 
-    @pl.when(b == 0)
-    def _():
-        for columns in tiles:
-            acc[:, columns] = product(columns)
-
-    @pl.when(b != 0)
-    def _():
-        for columns in tiles:
-            total = acc[:, columns] + product(columns)
-            if plan.batches > 2:
-                acc[:, columns] = total
-            out_f[:, columns] = total[:LANES].astype(out_f.dtype)
-            out_b[:, columns] = total[LANES:].astype(out_b.dtype)
+    def product(b, columns):
+        return jnp.dot(act[b], grad[b, :, columns], preferred_element_type=jnp.float32)
+
+    for b in range(plan.batches):
+        if b == 1:
+            for copy in copies:
+                copy.wait()
+            for columns in tiles:
+                acc[:, columns] = product(0, columns)
+        for j in range(count):
+            spec[b * count + j] = to_spectrum(
+                direct, x_ref[b, j * each : j * each + POINTS, :]
+            )
+        for j in range(count):
+            slot = b * count + j
+            spectral_product(spec, taps, parts, slot)
+            rows = min(each, plan.ext - j * each)
+            conv_ref[b, j * each : j * each + rows, :] = from_spectrum(
+                inverse, rows, parts, slot
+            )
+        for i in range(cf // LANES):
+            for side in range(2):
+                lanes = slice(side * LANES, (side + 1) * LANES)
+                begin = gh + i * LANES
+                conv = conv_ref[b, begin : begin + LANES, lanes]
+                pre = gain_ref[side][...] * conv + bias_ref[side][...]
+                position = lax.broadcasted_iota(jnp.int32, (LANES, LANES), 0) + (
+                    offset + i * LANES
+                )
+                value = jnp.where(position < info[3 + b], pre * sigmoid(pre), 0.0)
+                act[b, lanes, i * LANES : (i + 1) * LANES] = value.T.astype(jnp.bfloat16)
+
+    for columns in tiles:
+        total = acc[:, columns] + product(1, columns)
+        out_f[:, columns] = total[:LANES].astype(out_f.dtype)
+        out_b[:, columns] = total[LANES:].astype(out_b.dtype)
 
 
 def pair_specs(plan, step, shape, index):
@@ -341,17 +346,17 @@
     fixed = lambda b, info: (0, 0)
     direct, inverse, t_conv = consts[:3]
     wide = 2 * LANES
-    slots = plan.conv_windows[1]
+    slots = bt * plan.conv_windows[1]
     specs = functools.partial(pair_specs, plan, step)
-    frames, halo = (1, plan.frames, LANES), (1, plan.xhalo, LANES)
-    by_batch = lambda b, block: (b, 0, block)
-    by_chip = lambda b, block: (b, 0, block // CORES)
+    frames, halo = (bt, plan.frames, LANES), (bt, plan.xhalo, LANES)
+    by_batch = lambda b, block: (0, 0, block)
+    by_chip = lambda b, block: (0, 0, block // CORES)
     x_rows = plan.window_rows(plan.conv_windows)
     return pl.pallas_call(
         functools.partial(conv_body, plan),
         grid_spec=pltpu.PrefetchScalarGridSpec(
             num_scalar_prefetch=1,
-            grid=(bt,),
+            grid=(1,),
             in_specs=specs(frames, by_batch)
             + specs(frames, by_batch)
             + specs(halo, by_chip)
@@ -360,10 +365,10 @@
             + specs((1, LANES), flat)
             + specs((1, LANES), flat)
             + [whole(direct), whole(inverse), whole(t_conv)]
-            + [pl.BlockSpec((1, plan.frames, plan.width), lambda b, info: (b, 0, 0))] * 2,
+            + [pl.BlockSpec(memory_space=pl.ANY)] * 2,
             out_specs=[
-                pl.BlockSpec((1, plan.ext, wide), lambda b, info: (b, 0, 0)),
-                pl.BlockSpec((1, x_rows, wide), lambda b, info: (b, 0, 0)),
+                pl.BlockSpec((bt, plan.ext, wide), lambda b, info: (0, 0, 0)),
+                pl.BlockSpec((bt, x_rows, wide), lambda b, info: (0, 0, 0)),
                 pl.BlockSpec((LANES, plan.width), fixed),
                 pl.BlockSpec((LANES, plan.width), fixed),
             ],
@@ -371,8 +376,10 @@
                 pltpu.VMEM((slots, POINTS, wide), jnp.float32),
                 pltpu.VMEM((POINTS, wide), jnp.float32),
                 pltpu.VMEM((slots, POINTS, wide), jnp.bfloat16),
-                pltpu.VMEM((wide, plan.chip_frames), jnp.bfloat16),
+                pltpu.VMEM((bt, wide, plan.chip_frames), jnp.bfloat16),
                 pltpu.VMEM((wide, plan.width), jnp.float32),
+                pltpu.VMEM((bt, plan.chip_frames, plan.width), jnp.bfloat16),
+                pltpu.SemaphoreType.DMA((bt, 2)),
             ],
         ),
         out_shape=[

time: 138 us -> 138 us (level)
  no operation moved by 1% of the time
where the time goes in v1:
time: 138 us; the launch traced here: 137 us
  Pallas kernels  60.1 us (44%)
  starting transfers between devices  33.2 us (24%)
  waiting for transfers between devices  31.6 us (23%)
  local copies, waits for them, and re-layouts  6.83 us (5%)
  other arithmetic  3.34 us (2%)
  between operations  1.83 us (1%)
    pallas_call x4, Pallas kernels, conv_call(): pl.pallas_call(functools.partial(conv_body, plan), grid_spec=pltpu.Prefet...  29.2 us
    pallas_call x2, Pallas kernels, back_call(): pl.pallas_call(functools.partial(back_body, plan, steps, earlier, sources...  24.8 us
    ppermute x4, waiting for transfers between devices, weight_round(): going[0] = lax.ppermute(going[0], 'shard', forward)  18.8 us
    ppermute x3, starting transfers between devices, sum_round(): lax.ppermute(send[0], 'shard', forward)  9.47 us
    ppermute x4, starting transfers between devices, weight_round(): going[0] = lax.ppermute(going[0], 'shard', forward)  6.79 us
    ppermute x1, waiting for transfers between devices, ring_shards(): xb = lax.ppermute(x_far, 'shard', plan.edges_like())  6.02 us
    all_to_all x1, starting transfers between devices, ring_shards(): shares = lax.all_to_all(stats, 'shard', 0, 0, axis_index_groups=groups)  5.73 us
    ppermute x3, starting transfers between devices, ring_shards(): lax.ppermute(jnp.concatenate([around[d] for d in distances], 0), ('groups...  4.7 us
  transfers between devices with their start and end apart: 25, of which 6 were waited for; matrix products, arithmetic and copies ran while one was open for 4% of the time, Pallas kernels for 39%

profile of v1, /device:TPU:0, one launch (start us, length us, event | category | flops | bytes accessed | tf_op | source)
XLA Modules:
  0.0 136.9 jit_solution(6019674822775632412)
XLA Ops:
  1.3 1.9 %edge.1 = (bf16[2,64,1024]{2,1,0:T(8,128)(2,1)}, bf16[2,32,1024]{2,1,0:T(8,128)(2,1)}) custom-call(bf16[2,256,2048]{2,1,0:T(8,128)(2,1)} %refs_1_.7, bf16[2,256,2048]{2,1,0:T(8,128)(2,1)} %refs_1_.7, bf16[2,256,2048]{2,1,0:T(8,128)(2,1)} %refs_0_.11, bf16[2,256,2048]{2,1,0:T(8,128)(2,1)} %refs_0_.11), custom_call_target="tpu_custom_call" | custom-call | bytes 3600000 | tf_op jit(solution)/shard_map/edge/pallas_call | solution.py:712
  8.0 6.0 %collective-permute-done.1.refs_6_.refs_7_ = bf16[2,32,1024]{2,1,0:T(8,128)(2,1)S(1)} collective-permute-done((bf16[2,32,1024]{2,1,0:T(8,128)(2,1)}, bf16[2,32,1024]{2,1,0:T(8,128)(2,1)S(1)}, u32[]{:S(2)}, u32[]{:S(2)}) %collective-permute-start.1) | collective-permute-done | bytes 131104 | tf_op jit(solution)/shard_map/ppermute | solution.py:745
  15.4 7.1 %conv.4 = (f32[2,544,256]{2,1,0:T(8,128)}, bf16[2,640,256]{2,1,0:T(8,128)(2,1)}, bf16[128,2048]{1,0:T(8,128)(2,1)}, bf16[128,2048]{1,0:T(8,128)(2,1)}) custom-call(s32[13]{0:T(128)} %concatenate.12.info, bf16[2,256,2048]{2,1,0:T(8,128)(2,1)} %refs_1_.7, bf16[2,256,2048]{2,1,0:T(8,128)(2,1)} %refs_1_.7, bf16[2,256,2048]{2,1,0:T(8,128)(2,1)} %copy-done, ...), custom_call_target="tpu_custom_call" | custom-call | bytes 21600000 | tf_op jit(solution)/shard_map/conv/pallas_call | solution.py:355
  22.6 6.0 %collective-permute-start.4 = (bf16[128,2048]{1,0:T(8,128)(2,1)}, bf16[128,2048]{1,0:T(8,128)(2,1)S(1)}, u32[]{:S(2)}, u32[]{:S(2)}) collective-permute-start(bf16[128,2048]{1,0:T(8,128)(2,1)} %get-tuple-element.59), channel_id=1, source_target_pairs={{0,4},{4,8},{8,12},{12,14},{14,10},{10,6},{6,2},{2,0},{1,5},{5,9},... | collective-permute-start | bytes 1572872 | tf_op jit(solution)/shard_map/ppermute | solution.py:779
  28.6 2.1 %collective-permute-start.12 = (bf16[64,2048]{1,0:T(8,128)(2,1)S(1)}, bf16[64,2048]{1,0:T(8,128)(2,1)S(1)}, u32[]{:S(2)}, u32[]{:S(2)}) collective-permute-start(bf16[64,2048]{1,0:T(8,128)(2,1)S(1)} %constant_dynamic-slice_fusion), channel_id=1, source_target_pairs={{0,4},{4,8},{8,12},{12,14},{14,10},{10,6},{6,2},{2,0},{1,5},{5,9},... | collective-permute-start | bytes 786440 | tf_op jit(solution)/shard_map/ppermute | solution.py:758
  30.7 7.4 %conv.5 = (f32[2,544,256]{2,1,0:T(8,128)}, bf16[2,640,256]{2,1,0:T(8,128)(2,1)}, f32[128,2048]{1,0:T(8,128)}, f32[128,2048]{1,0:T(8,128)}) custom-call(s32[13]{0:T(128)} %concatenate.12.info, bf16[2,256,2048]{2,1,0:T(8,128)(2,1)} %refs_1_.7, bf16[2,256,2048]{2,1,0:T(8,128)(2,1)} %refs_1_.7, bf16[2,256,2048]{2,1,0:T(8,128)(2,1)} %copy-done, ...), custom_call_target="tpu_custom_call" | custom-call | bytes 21600000 | tf_op jit(solution)/shard_map/conv/pallas_call | solution.py:355
  38.1 6.7 %collective-permute-done.12.refs_23_ = bf16[64,2048]{1,0:T(8,128)(2,1)S(1)} collective-permute-done((bf16[64,2048]{1,0:T(8,128)(2,1)S(1)}, bf16[64,2048]{1,0:T(8,128)(2,1)S(1)}, u32[]{:S(2)}, u32[]{:S(2)}) %collective-permute-start.12) | collective-permute-done | bytes 262176 | tf_op jit(solution)/shard_map/ppermute | solution.py:758
  44.8 2.1 %collective-permute-done.11.refs_22_ = bf16[64,2048]{1,0:T(8,128)(2,1)S(1)} collective-permute-done((bf16[64,2048]{1,0:T(8,128)(2,1)S(1)}, bf16[64,2048]{1,0:T(8,128)(2,1)S(1)}, u32[]{:S(2)}, u32[]{:S(2)}) %collective-permute-start.11) | collective-permute-done | bytes 262176 | tf_op jit(solution)/shard_map/ppermute | solution.py:761
  47.0 1.6 %collective-permute-start.15 = (bf16[64,2048]{1,0:T(8,128)(2,1)S(1)}, bf16[64,2048]{1,0:T(8,128)(2,1)S(1)}, u32[]{:S(2)}, u32[]{:S(2)}) collective-permute-start(bf16[64,2048]{1,0:T(8,128)(2,1)S(1)} %collective-permute-done.12.refs_23_), channel_id=1, source_target_pairs={{0,4},{4,8},{8,12},{12,14},{14,10},{10,6},{6,2},{2,0},{1,5},{5,9},... | collective-permute-start | bytes 786440 | tf_op jit(solution)/shard_map/ppermute | solution.py:758
  49.0 7.4 %conv.6 = (f32[2,544,256]{2,1,0:T(8,128)}, bf16[2,640,256]{2,1,0:T(8,128)(2,1)}, f32[128,2048]{1,0:T(8,128)}, f32[128,2048]{1,0:T(8,128)}) custom-call(s32[13]{0:T(128)} %concatenate.12.info, bf16[2,256,2048]{2,1,0:T(8,128)(2,1)} %refs_1_.7, bf16[2,256,2048]{2,1,0:T(8,128)(2,1)} %refs_1_.7, bf16[2,256,2048]{2,1,0:T(8,128)(2,1)} %copy-done, ...), custom_call_target="tpu_custom_call" | custom-call | bytes 21600000 | tf_op jit(solution)/shard_map/conv/pallas_call | solution.py:355
  56.5 1.6 %collective-permute-start.6 = (bf16[128,2048]{1,0:T(8,128)(2,1)S(1)}, bf16[128,2048]{1,0:T(8,128)(2,1)S(1)}, u32[]{:S(2)}, u32[]{:S(2)}) collective-permute-start(bf16[128,2048]{1,0:T(8,128)(2,1)S(1)} %add_convert_fusion.4), channel_id=1, source_target_pairs={{0,4},{4,8},{8,12},{12,14},{14,10},{10,6},{6,2},{2,0},{1,5},{5,9},... | collective-permute-start | bytes 1572872 | tf_op jit(solution)/shard_map/ppermute | solution.py:779
  58.8 1.6 %collective-permute-start.18 = (bf16[64,2048]{1,0:T(8,128)(2,1)S(1)}, bf16[64,2048]{1,0:T(8,128)(2,1)S(1)}, u32[]{:S(2)}, u32[]{:S(2)}) collective-permute-start(bf16[64,2048]{1,0:T(8,128)(2,1)S(1)} %collective-permute-done.15.refs_21_), channel_id=1, source_target_pairs={{0,4},{4,8},{8,12},{12,14},{14,10},{10,6},{6,2},{2,0},{1,5},{5,9},... | collective-permute-start | bytes 786440 | tf_op jit(solution)/shard_map/ppermute | solution.py:758
  60.9 1.6 %collective-permute-start.13 = (bf16[128,2048]{1,0:T(8,128)(2,1)S(1)}, bf16[128,2048]{1,0:T(8,128)(2,1)S(1)}, u32[]{:S(2)}, u32[]{:S(2)}) collective-permute-start(bf16[128,2048]{1,0:T(8,128)(2,1)S(1)} %pad_maximum_fusion.1), channel_id=1, source_target_pairs={{0,16},{1,17},{2,18},{3,19},{4,20},{5,21},{6,22},{7,23},{8,24},{9,... | collective-permute-start | bytes 1572872 | tf_op jit(solution)/shard_map/ppermute | solution.py:822
  62.6 12.0 %collective-permute-done.18.refs_24_ = bf16[64,2048]{1,0:T(8,128)(2,1)S(1)} collective-permute-done((bf16[64,2048]{1,0:T(8,128)(2,1)S(1)}, bf16[64,2048]{1,0:T(8,128)(2,1)S(1)}, u32[]{:S(2)}, u32[]{:S(2)}) %collective-permute-start.18) | collective-permute-done | bytes 262176 | tf_op jit(solution)/shard_map/ppermute | solution.py:758
  77.6 7.4 %conv.7 = (f32[2,544,256]{2,1,0:T(8,128)}, bf16[2,640,256]{2,1,0:T(8,128)(2,1)}, f32[128,2048]{1,0:T(8,128)}, f32[128,2048]{1,0:T(8,128)}) custom-call(s32[13]{0:T(128)} %concatenate.12.info, bf16[2,256,2048]{2,1,0:T(8,128)(2,1)} %refs_1_.7, bf16[2,256,2048]{2,1,0:T(8,128)(2,1)} %refs_1_.7, bf16[2,256,2048]{2,1,0:T(8,128)(2,1)} %copy-done, ...), custom_call_target="tpu_custom_call" | custom-call | bytes 21600000 | tf_op jit(solution)/shard_map/conv/pallas_call | solution.py:355
  85.2 1.8 %collective-permute-start.8 = (bf16[128,2048]{1,0:T(8,128)(2,1)S(1)}, bf16[128,2048]{1,0:T(8,128)(2,1)S(1)}, u32[]{:S(2)}, u32[]{:S(2)}) collective-permute-start(bf16[128,2048]{1,0:T(8,128)(2,1)S(1)} %add_convert_fusion.2), channel_id=1, source_target_pairs={{0,4},{4,8},{8,12},{12,14},{14,10},{10,6},{6,2},{2,0},{1,5},{5,9},... | collective-permute-start | bytes 1572872 | tf_op jit(solution)/shard_map/ppermute | solution.py:779
  88.4 1.6 %collective-permute-start.20 = (bf16[192,2048]{1,0:T(8,128)(2,1)S(1)}, bf16[192,2048]{1,0:T(8,128)(2,1)S(1)}, u32[]{:S(2)}, u32[]{:S(2)}) collective-permute-start(bf16[192,2048]{1,0:T(8,128)(2,1)S(1)} %pad_maximum_fusion), channel_id=1, source_target_pairs={{0,16},{1,17},{2,18},{3,19},{4,20},{5,21},{6,22},{7,23},{8,24},{9,... | collective-permute-start | bytes 2359304 | tf_op jit(solution)/shard_map/ppermute | solution.py:822
  90.9 12.3 %back.2 = (bf16[2,2,256,256]{3,2,1,0:T(8,128)(2,1)}, bf16[2,2,256,256]{3,2,1,0:T(8,128)(2,1)}, f32[2,40,256]{2,1,0:T(8,128)}) custom-call(s32[13]{0:T(128)} %concatenate.12.info, bf16[2,256,2048]{2,1,0:T(8,128)(2,1)} %refs_0_.11, bf16[2,256,2048]{2,1,0:T(8,128)(2,1)} %collective-permute-done.3.refs_18_.refs_1_, bf16[2,64,1024]{2,1,0:T(8,128)(2,1)} %copy-done.1, ...), custom_call_target="tpu_custom_call" | custom-call | bytes 43200000 | tf_op jit(solution)/shard_map/back/pallas_call | solution.py:601
  103.7 1.8 %collective-permute-start.23 = (bf16[128,2048]{1,0:T(8,128)(2,1)S(1)}, bf16[128,2048]{1,0:T(8,128)(2,1)S(1)}, u32[]{:S(2)}, u32[]{:S(2)}) collective-permute-start(bf16[128,2048]{1,0:T(8,128)(2,1)S(1)} %add_convert_fusion), channel_id=1, source_target_pairs={{0,4},{4,8},{8,12},{12,14},{14,10},{10,6},{6,2},{2,0},{1,5},{5,9},... | collective-permute-start | bytes 1572872 | tf_op jit(solution)/shard_map/ppermute | solution.py:852
  105.6 2.7 %collective-permute-done.20.refs_22_ = bf16[192,2048]{1,0:T(8,128)(2,1)S(1)} collective-permute-done((bf16[192,2048]{1,0:T(8,128)(2,1)S(1)}, bf16[192,2048]{1,0:T(8,128)(2,1)S(1)}, u32[]{:S(2)}, u32[]{:S(2)}) %collective-permute-start.20) | collective-permute-done | bytes 786464 | tf_op jit(solution)/shard_map/ppermute | solution.py:822
  109.2 12.5 %back.3 = (bf16[2,2,256,256]{3,2,1,0:T(8,128)(2,1)}, bf16[2,2,256,256]{3,2,1,0:T(8,128)(2,1)}, f32[8,40,128]{2,1,0:T(8,128)}) custom-call(s32[13]{0:T(128)} %concatenate.12.info, bf16[2,256,2048]{2,1,0:T(8,128)(2,1)} %refs_0_.11, bf16[2,256,2048]{2,1,0:T(8,128)(2,1)} %collective-permute-done.3.refs_18_.refs_1_, bf16[2,64,1024]{2,1,0:T(8,128)(2,1)} %copy-done.1, ...), custom_call_target="tpu_custom_call" | custom-call | bytes 43200000 | tf_op jit(solution)/shard_map/back/pallas_call | solution.py:601
  121.8 5.7 %all-to-all-start = ((f32[8,40,128]{2,1,0:T(8,128)}), f32[8,40,128]{2,1,0:T(8,128)S(1)}, u32[]{:S(2)}, u32[]{:S(2)}) async-start(f32[8,40,128]{2,1,0:T(8,128)} %get-tuple-element.94), calls=%async_computation | async-start | bytes 327680 | tf_op jit(solution)/shard_map/all_to_all | solution.py:855
  128.6 4.1 %place.1 = bf16[2,256,2048]{2,1,0:T(8,128)(2,1)} custom-call(s32[13]{0:T(128)} %concatenate.12.info, bf16[2,2,256,256]{3,2,1,0:T(8,128)(2,1)} %get-tuple-element.82.refs_0_, bf16[2,2,256,256]{3,2,1,0:T(8,128)(2,1)} %copy-done.22, bf16[2,2,256,256]{3,2,1,0:T(8,128)(2,1)} %get-tuple-element.97.refs_2_, bf16[2,2,256,256]{3,2,1,0:T(8,128)(2,1)} %copy-done.23), custom_call_target="tpu_custom_call" | custom-call | bytes 10800000 | tf_op jit(solution)/shard_map/place/pallas_call | solution.py:666
  133.8 1.9 %all-to-all-done = f32[8,40,128]{2,1,0:T(8,128)S(1)} async-done(((f32[8,40,128]{2,1,0:T(8,128)}), f32[8,40,128]{2,1,0:T(8,128)S(1)}, u32[]{:S(2)}, u32[]{:S(2)}) %all-to-all-start) | async-done | bytes 163872 | tf_op jit(solution)/shard_map/all_to_all | solution.py:855
  (108 shorter events, 18.0 us)
Async XLA Ops:
  0.7 13.3 %collective-permute-start.2 = (bf16[2,256,2048]{2,1,0:T(8,128)(2,1)}, bf16[2,256,2048]{2,1,0:T(8,128)(2,1)S(1)}, u32[]{:S(2)}, u32[]{:S(2)}) collective-permute-start(bf16[2,256,2048]{2,1,0:T(8,128)(2,1)} %refs_1_.7), channel_id=1, source_target_pairs={{0,1},{1,0},{2,3},{3,2},{4,5},{5,4},{6,7},{7,6},{8,9},{9,8},{10,11... | collective-permute-start | bytes 6291464 | tf_op jit(solution)/shard_map/ppermute | solution.py:746
  1.2 12.8 %collective-permute-start.3 = (bf16[2,256,2048]{2,1,0:T(8,128)(2,1)}, bf16[2,256,2048]{2,1,0:T(8,128)(2,1)}, u32[]{:S(2)}, u32[]{:S(2)}) collective-permute-start(bf16[2,256,2048]{2,1,0:T(8,128)(2,1)} %refs_0_.11), channel_id=1, source_target_pairs={{0,1},{1,0},{2,3},{3,2},{4,5},{5,4},{6,7},{7,6},{8,9},{9,8},{10,11... | collective-permute-start | bytes 6291464 | tf_op jit(solution)/shard_map/ppermute | solution.py:747
  3.2 10.8 %collective-permute-start = (bf16[2,64,1024]{2,1,0:T(8,128)(2,1)}, bf16[2,64,1024]{2,1,0:T(8,128)(2,1)S(1)}, u32[]{:S(2)}, u32[]{:S(2)}) collective-permute-start(bf16[2,64,1024]{2,1,0:T(8,128)(2,1)} %get-tuple-element.53), channel_id=1, source_target_pairs={{1,2},{2,1},{3,4},{4,3},{5,6},{6,5},{7,8},{8,7},{9,10},{10,9},{11,... | collective-permute-start | bytes 786440 | tf_op jit(solution)/shard_map/ppermute | solution.py:744
  3.9 10.1 %collective-permute-start.1 = (bf16[2,32,1024]{2,1,0:T(8,128)(2,1)}, bf16[2,32,1024]{2,1,0:T(8,128)(2,1)S(1)}, u32[]{:S(2)}, u32[]{:S(2)}) collective-permute-start(bf16[2,32,1024]{2,1,0:T(8,128)(2,1)} %get-tuple-element.54), channel_id=1, source_target_pairs={{1,3},{2,0},{3,5},{4,2},{5,7},{6,4},{7,9},{8,6},{9,11},{10,8},{11,... | collective-permute-start | bytes 393224 | tf_op jit(solution)/shard_map/ppermute | solution.py:745
  22.6 33.8 %collective-permute-start.4 = (bf16[128,2048]{1,0:T(8,128)(2,1)}, bf16[128,2048]{1,0:T(8,128)(2,1)S(1)}, u32[]{:S(2)}, u32[]{:S(2)}) collective-permute-start(bf16[128,2048]{1,0:T(8,128)(2,1)} %get-tuple-element.59), channel_id=1, source_target_pairs={{0,4},{4,8},{8,12},{12,14},{14,10},{10,6},{6,2},{2,0},{1,5},{5,9},... | collective-permute-start | bytes 1572872 | tf_op jit(solution)/shard_map/ppermute | solution.py:779
  28.6 27.8 %collective-permute-start.5 = (bf16[128,2048]{1,0:T(8,128)(2,1)}, bf16[128,2048]{1,0:T(8,128)(2,1)S(1)}, u32[]{:S(2)}, u32[]{:S(2)}) collective-permute-start(bf16[128,2048]{1,0:T(8,128)(2,1)} %get-tuple-element.65), channel_id=1, source_target_pairs={{4,0},{8,4},{12,8},{14,12},{10,14},{6,10},{2,6},{0,2},{5,1},{9,5},... | collective-permute-start | bytes 1572872 | tf_op jit(solution)/shard_map/ppermute | solution.py:779
  28.6 16.2 %collective-permute-start.12 = (bf16[64,2048]{1,0:T(8,128)(2,1)S(1)}, bf16[64,2048]{1,0:T(8,128)(2,1)S(1)}, u32[]{:S(2)}, u32[]{:S(2)}) collective-permute-start(bf16[64,2048]{1,0:T(8,128)(2,1)S(1)} %constant_dynamic-slice_fusion), channel_id=1, source_target_pairs={{0,4},{4,8},{8,12},{12,14},{14,10},{10,6},{6,2},{2,0},{1,5},{5,9},... | collective-permute-start | bytes 786440 | tf_op jit(solution)/shard_map/ppermute | solution.py:758
  30.7 16.2 %collective-permute-start.11 = (bf16[64,2048]{1,0:T(8,128)(2,1)S(1)}, bf16[64,2048]{1,0:T(8,128)(2,1)S(1)}, u32[]{:S(2)}, u32[]{:S(2)}) collective-permute-start(bf16[64,2048]{1,0:T(8,128)(2,1)S(1)} %constant_dynamic-slice_fusion), channel_id=1, source_target_pairs={{4,0},{8,4},{12,8},{14,12},{10,14},{6,10},{2,6},{0,2},{5,1},{9,5},... | collective-permute-start | bytes 786440 | tf_op jit(solution)/shard_map/ppermute | solution.py:761
  47.0 11.8 %collective-permute-start.15 = (bf16[64,2048]{1,0:T(8,128)(2,1)S(1)}, bf16[64,2048]{1,0:T(8,128)(2,1)S(1)}, u32[]{:S(2)}, u32[]{:S(2)}) collective-permute-start(bf16[64,2048]{1,0:T(8,128)(2,1)S(1)} %collective-permute-done.12.refs_23_), channel_id=1, source_target_pairs={{0,4},{4,8},{8,12},{12,14},{14,10},{10,6},{6,2},{2,0},{1,5},{5,9},... | collective-permute-start | bytes 786440 | tf_op jit(solution)/shard_map/ppermute | solution.py:758
  48.5 10.2 %collective-permute-start.14 = (bf16[64,2048]{1,0:T(8,128)(2,1)S(1)}, bf16[64,2048]{1,0:T(8,128)(2,1)S(1)}, u32[]{:S(2)}, u32[]{:S(2)}) collective-permute-start(bf16[64,2048]{1,0:T(8,128)(2,1)S(1)} %collective-permute-done.11.refs_22_), channel_id=1, source_target_pairs={{4,0},{8,4},{12,8},{14,12},{10,14},{6,10},{2,6},{0,2},{5,1},{9,5},... | collective-permute-start | bytes 786440 | tf_op jit(solution)/shard_map/ppermute | solution.py:761
  56.5 28.5 %collective-permute-start.6 = (bf16[128,2048]{1,0:T(8,128)(2,1)S(1)}, bf16[128,2048]{1,0:T(8,128)(2,1)S(1)}, u32[]{:S(2)}, u32[]{:S(2)}) collective-permute-start(bf16[128,2048]{1,0:T(8,128)(2,1)S(1)} %add_convert_fusion.4), channel_id=1, source_target_pairs={{0,4},{4,8},{8,12},{12,14},{14,10},{10,6},{6,2},{2,0},{1,5},{5,9},... | collective-permute-start | bytes 1572872 | tf_op jit(solution)/shard_map/ppermute | solution.py:779
  58.3 26.8 %collective-permute-start.7 = (bf16[128,2048]{1,0:T(8,128)(2,1)S(1)}, bf16[128,2048]{1,0:T(8,128)(2,1)S(1)}, u32[]{:S(2)}, u32[]{:S(2)}) collective-permute-start(bf16[128,2048]{1,0:T(8,128)(2,1)S(1)} %add_convert_fusion.3), channel_id=1, source_target_pairs={{4,0},{8,4},{12,8},{14,12},{10,14},{6,10},{2,6},{0,2},{5,1},{9,5},... | collective-permute-start | bytes 1572872 | tf_op jit(solution)/shard_map/ppermute | solution.py:779
  58.8 15.8 %collective-permute-start.18 = (bf16[64,2048]{1,0:T(8,128)(2,1)S(1)}, bf16[64,2048]{1,0:T(8,128)(2,1)S(1)}, u32[]{:S(2)}, u32[]{:S(2)}) collective-permute-start(bf16[64,2048]{1,0:T(8,128)(2,1)S(1)} %collective-permute-done.15.refs_21_), channel_id=1, source_target_pairs={{0,4},{4,8},{8,12},{12,14},{14,10},{10,6},{6,2},{2,0},{1,5},{5,9},... | collective-permute-start | bytes 786440 | tf_op jit(solution)/shard_map/ppermute | solution.py:758
  60.4 15.7 %collective-permute-start.17 = (bf16[64,2048]{1,0:T(8,128)(2,1)S(1)}, bf16[64,2048]{1,0:T(8,128)(2,1)S(1)}, u32[]{:S(2)}, u32[]{:S(2)}) collective-permute-start(bf16[64,2048]{1,0:T(8,128)(2,1)S(1)} %collective-permute-done.14.refs_25_), channel_id=1, source_target_pairs={{4,0},{8,4},{12,8},{14,12},{10,14},{6,10},{2,6},{0,2},{5,1},{9,5},... | collective-permute-start | bytes 786440 | tf_op jit(solution)/shard_map/ppermute | solution.py:761
  60.9 27.4 %collective-permute-start.13 = (bf16[128,2048]{1,0:T(8,128)(2,1)S(1)}, bf16[128,2048]{1,0:T(8,128)(2,1)S(1)}, u32[]{:S(2)}, u32[]{:S(2)}) collective-permute-start(bf16[128,2048]{1,0:T(8,128)(2,1)S(1)} %pad_maximum_fusion.1), channel_id=1, source_target_pairs={{0,16},{1,17},{2,18},{3,19},{4,20},{5,21},{6,22},{7,23},{8,24},{9,... | collective-permute-start | bytes 1572872 | tf_op jit(solution)/shard_map/ppermute | solution.py:822
  74.6 15.4 %collective-permute-start.16 = (bf16[128,2048]{1,0:T(8,128)(2,1)S(1)}, bf16[128,2048]{1,0:T(8,128)(2,1)S(1)}, u32[]{:S(2)}, u32[]{:S(2)}) collective-permute-start(bf16[128,2048]{1,0:T(8,128)(2,1)S(1)} %pad_maximum_fusion.2), channel_id=1, source_target_pairs={{0,16},{1,17},{2,18},{3,19},{4,20},{5,21},{6,22},{7,23},{8,24},{9,... | collective-permute-start | bytes 1572872 | tf_op jit(solution)/shard_map/ppermute | solution.py:822
  76.1 12.1 %collective-permute-start.19 = (bf16[64,2048]{1,0:T(8,128)(2,1)S(1)}, bf16[64,2048]{1,0:T(8,128)(2,1)S(1)}, u32[]{:S(2)}, u32[]{:S(2)}) collective-permute-start(bf16[64,2048]{1,0:T(8,128)(2,1)S(1)} %collective-permute-done.18.refs_24_), channel_id=1, source_target_pairs={{0,4},{4,8},{8,12},{12,14},{14,10},{10,6},{6,2},{2,0},{1,5},{5,9},... | collective-permute-start | bytes 786440 | tf_op jit(solution)/shard_map/ppermute | solution.py:758
  85.2 18.4 %collective-permute-start.8 = (bf16[128,2048]{1,0:T(8,128)(2,1)S(1)}, bf16[128,2048]{1,0:T(8,128)(2,1)S(1)}, u32[]{:S(2)}, u32[]{:S(2)}) collective-permute-start(bf16[128,2048]{1,0:T(8,128)(2,1)S(1)} %add_convert_fusion.2), channel_id=1, source_target_pairs={{0,4},{4,8},{8,12},{12,14},{14,10},{10,6},{6,2},{2,0},{1,5},{5,9},... | collective-permute-start | bytes 1572872 | tf_op jit(solution)/shard_map/ppermute | solution.py:779
  87.9 15.7 %collective-permute-start.9 = (bf16[128,2048]{1,0:T(8,128)(2,1)}, bf16[128,2048]{1,0:T(8,128)(2,1)S(1)}, u32[]{:S(2)}, u32[]{:S(2)}) collective-permute-start(bf16[128,2048]{1,0:T(8,128)(2,1)} %add_convert_fusion.1), channel_id=1, source_target_pairs={{4,0},{8,4},{12,8},{14,12},{10,14},{6,10},{2,6},{0,2},{5,1},{9,5},... | collective-permute-start | bytes 1572872 | tf_op jit(solution)/shard_map/ppermute | solution.py:779
  88.4 20.0 %collective-permute-start.20 = (bf16[192,2048]{1,0:T(8,128)(2,1)S(1)}, bf16[192,2048]{1,0:T(8,128)(2,1)S(1)}, u32[]{:S(2)}, u32[]{:S(2)}) collective-permute-start(bf16[192,2048]{1,0:T(8,128)(2,1)S(1)} %pad_maximum_fusion), channel_id=1, source_target_pairs={{0,16},{1,17},{2,18},{3,19},{4,20},{5,21},{6,22},{7,23},{8,24},{9,... | collective-permute-start | bytes 2359304 | tf_op jit(solution)/shard_map/ppermute | solution.py:822
  103.3 24.3 %collective-permute-start.21 = (bf16[2,2,256,256]{3,2,1,0:T(8,128)(2,1)}, bf16[2,2,256,256]{3,2,1,0:T(8,128)(2,1)S(1)}, u32[]{:S(2)}, u32[]{:S(2)}) collective-permute-start(bf16[2,2,256,256]{3,2,1,0:T(8,128)(2,1)} %get-tuple-element.96), channel_id=1, source_target_pairs={{0,1},{1,0},{2,3},{3,2},{4,5},{5,4},{6,7},{7,6},{8,9},{9,8},{10,11... | collective-permute-start | bytes 1572872 | tf_op jit(solution)/shard_map/ppermute | solution.py:851
  103.7 23.8 %collective-permute-start.23 = (bf16[128,2048]{1,0:T(8,128)(2,1)S(1)}, bf16[128,2048]{1,0:T(8,128)(2,1)S(1)}, u32[]{:S(2)}, u32[]{:S(2)}) collective-permute-start(bf16[128,2048]{1,0:T(8,128)(2,1)S(1)} %add_convert_fusion), channel_id=1, source_target_pairs={{0,4},{4,8},{8,12},{12,14},{14,10},{10,6},{6,2},{2,0},{1,5},{5,9},... | collective-permute-start | bytes 1572872 | tf_op jit(solution)/shard_map/ppermute | solution.py:852
  121.7 5.8 %collective-permute-start.22 = (bf16[2,2,256,256]{3,2,1,0:T(8,128)(2,1)}, bf16[2,2,256,256]{3,2,1,0:T(8,128)(2,1)S(1)}, u32[]{:S(2)}, u32[]{:S(2)}) collective-permute-start(bf16[2,2,256,256]{3,2,1,0:T(8,128)(2,1)} %get-tuple-element.98), channel_id=1, source_target_pairs={{0,1},{1,0},{2,3},{3,2},{4,5},{5,4},{6,7},{7,6},{8,9},{9,8},{10,11... | collective-permute-start | bytes 1572872 | tf_op jit(solution)/shard_map/ppermute | solution.py:851
  121.8 13.8 %all-to-all-start = ((f32[8,40,128]{2,1,0:T(8,128)}), f32[8,40,128]{2,1,0:T(8,128)S(1)}, u32[]{:S(2)}, u32[]{:S(2)}) async-start(f32[8,40,128]{2,1,0:T(8,128)} %get-tuple-element.94), calls=%async_computation | async-start | bytes 327680 | tf_op jit(solution)/shard_map/all_to_all | solution.py:855
  (28 other events, 227.4 us)

commit v2 on v1

--- a/solution.py
+++ b/solution.py
@@ -801,7 +801,6 @@
     weight_round(4)
     send = sum_round(1, products[0], products[2][0])
     conv_step(3, after(info, products[2][0], *send))
-    send = sum_round(2, send, products[3][0])
 
     arrays = [proj_weight]
     source = {0: [(0, None, 0, LANES)]}
@@ -830,8 +829,6 @@
     calls = [(3, 2), (1, 0)]
     pieces, stats = [], None
     for steps in calls:
-        if steps == calls[-1]:
-            send = sum_round(3, send, pieces[0])
         order = after(info, products[-1][0], *send)
         used = sorted({a[0] for step in steps for d in pairs[step] for a in source[d]})
         sources = [
@@ -848,13 +845,14 @@
             taps, gain2, bias2, consts, stats, calls[0],
         )
         stats = stat
+        send = sum_round(2 if steps == calls[0] else 3, send, own)
         pieces += [own, lax.ppermute(given, "shard", plan.partners())]
-    recv_f = after(lax.ppermute(send[0], "shard", forward), stats)
-    proj_grad = (send[1] + recv_f.astype(jnp.float32)) * scale
     groups = [[CORES * p + c for p in range(plan.chips)] for c in range(CORES)]
     shares = lax.all_to_all(stats, "shard", 0, 0, axis_index_groups=groups)
     full = place_call(plan, calls, after(info, stats), pieces)
-    summed = jnp.sum(after(shares, full, proj_grad), axis=0) * scale
+    summed = jnp.sum(after(shares, full), axis=0) * scale
+    recv_f = after(lax.ppermute(send[0], "shard", forward), full, summed)
+    proj_grad = (send[1] + recv_f.astype(jnp.float32)) * scale
     return (
         full, proj_grad, summed[: plan.taps], summed[plan.tap_rows : plan.tap_rows + 2]
     )

time: 138 us -> 131 us (0.949)
  waiting for transfers between devices: 31.6 us -> 20.6 us
  starting transfers between devices: 33.2 us -> 36.6 us
    ppermute x4, waiting for transfers between devices: 18.8 us -> 7.19 us  [weight_round(): going[0] = lax.ppermute(going[0], 'shard', forward)]
    ppermute x4, starting transfers between devices: 6.79 us -> 13.4 us  [weight_round(): going[0] = lax.ppermute(going[0], 'shard', forward)]
    all_to_all x1, waiting for transfers between devices: 1.86 us -> 8.14 us  [ring_shards(): shares = lax.all_to_all(stats, 'shard', 0, 0, axis_index_groups=groups)]
    ppermute x3, starting transfers between devices: 9.47 us -> 3.94 us  [sum_round(): lax.ppermute(send[0], 'shard', forward)]
    ppermute x1, waiting for transfers between devices: 6.02 us -> 2.46 us  [ring_shards(): xb = lax.ppermute(x_far, 'shard', plan.edges_like())]
    ppermute x3, starting transfers between devices: 0.79 us -> 2.65 us  [sum_round(): lax.ppermute(send[1], 'shard', backward)]
    ppermute x3, starting transfers between devices: 0.91 us -> 2.71 us  [weight_round(): going[1] = lax.ppermute(going[1], 'shard', backward)]
    ppermute x3, waiting for transfers between devices: 2.12 us -> 0.33 us  [weight_round(): going[1] = lax.ppermute(going[1], 'shard', backward)]
  transfers between devices with their start and end apart: 25 -> 25, of which waited for: 6 -> 6; matrix products, arithmetic and copies ran while one was open for 4% -> 4% of each run, Pallas kernels for 39% -> 46%
where the time goes in v2:
time: 131 us; the launch traced here: 130 us
  Pallas kernels  60.3 us (46%)
  starting transfers between devices  36.6 us (28%)
  waiting for transfers between devices  20.6 us (16%)
  local copies, waits for them, and re-layouts  7.49 us (6%)
  other arithmetic  3.33 us (3%)
  between operations  1.82 us (1%)
    pallas_call x4, Pallas kernels, conv_call(): pl.pallas_call(functools.partial(conv_body, plan), grid_spec=pltpu.Prefet...  29.3 us
    pallas_call x2, Pallas kernels, back_call(): pl.pallas_call(functools.partial(back_body, plan, steps, earlier, sources...  25 us
    ppermute x4, starting transfers between devices, weight_round(): going[0] = lax.ppermute(going[0], 'shard', forward)  13.4 us
    all_to_all x1, waiting for transfers between devices, ring_shards(): shares = lax.all_to_all(stats, 'shard', 0, 0, axis_index_groups=groups)  8.14 us
    ppermute x4, waiting for transfers between devices, weight_round(): going[0] = lax.ppermute(going[0], 'shard', forward)  7.19 us
    all_to_all x1, starting transfers between devices, ring_shards(): shares = lax.all_to_all(stats, 'shard', 0, 0, axis_index_groups=groups)  4.93 us
    ppermute x3, starting transfers between devices, ring_shards(): lax.ppermute(jnp.concatenate([around[d] for d in distances], 0), ('groups...  4.56 us
    unnamed x54, local copies, waits for them, and re-layouts  4.29 us
  transfers between devices with their start and end apart: 25, of which 6 were waited for; matrix products, arithmetic and copies ran while one was open for 4% of the time, Pallas kernels for 46%

profile of v2, /device:TPU:0, one launch (start us, length us, event | category | flops | bytes accessed | tf_op | source)
XLA Modules:
  0.0 130.1 jit_solution(2343956185789048645)
XLA Ops:
  1.3 1.9 %edge.1 = (bf16[2,64,1024]{2,1,0:T(8,128)(2,1)}, bf16[2,32,1024]{2,1,0:T(8,128)(2,1)}) custom-call(bf16[2,256,2048]{2,1,0:T(8,128)(2,1)} %refs_1_.7, bf16[2,256,2048]{2,1,0:T(8,128)(2,1)} %refs_1_.7, bf16[2,256,2048]{2,1,0:T(8,128)(2,1)} %refs_0_.11, bf16[2,256,2048]{2,1,0:T(8,128)(2,1)} %refs_0_.11), custom_call_target="tpu_custom_call" | custom-call | bytes 3600000 | tf_op jit(solution)/shard_map/edge/pallas_call | solution.py:712
  5.2 6.3 %collective-permute-start.10 = (bf16[64,2048]{1,0:T(8,128)(2,1)S(1)}, bf16[64,2048]{1,0:T(8,128)(2,1)S(1)}, u32[]{:S(2)}, u32[]{:S(2)}) collective-permute-start(bf16[64,2048]{1,0:T(8,128)(2,1)S(1)} %constant_dynamic-slice_fusion), channel_id=1, source_target_pairs={{0,4},{4,8},{8,12},{12,14},{14,10},{10,6},{6,2},{2,0},{1,5},{5,9},... | collective-permute-start | bytes 786440 | tf_op jit(solution)/shard_map/ppermute | solution.py:758
  11.5 2.5 %collective-permute-done.1.refs_6_.refs_7_ = bf16[2,32,1024]{2,1,0:T(8,128)(2,1)S(1)} collective-permute-done((bf16[2,32,1024]{2,1,0:T(8,128)(2,1)}, bf16[2,32,1024]{2,1,0:T(8,128)(2,1)S(1)}, u32[]{:S(2)}, u32[]{:S(2)}) %collective-permute-start.1) | collective-permute-done | bytes 131104 | tf_op jit(solution)/shard_map/ppermute | solution.py:745
  14.0 2.7 %collective-permute-start.9 = (bf16[64,2048]{1,0:T(8,128)(2,1)S(1)}, bf16[64,2048]{1,0:T(8,128)(2,1)S(1)}, u32[]{:S(2)}, u32[]{:S(2)}) collective-permute-start(bf16[64,2048]{1,0:T(8,128)(2,1)S(1)} %constant_dynamic-slice_fusion), channel_id=1, source_target_pairs={{4,0},{8,4},{12,8},{14,12},{10,14},{6,10},{2,6},{0,2},{5,1},{9,5},... | collective-permute-start | bytes 786440 | tf_op jit(solution)/shard_map/ppermute | solution.py:761
  20.8 7.0 %conv.4 = (f32[2,544,256]{2,1,0:T(8,128)}, bf16[2,640,256]{2,1,0:T(8,128)(2,1)}, bf16[128,2048]{1,0:T(8,128)(2,1)}, bf16[128,2048]{1,0:T(8,128)(2,1)}) custom-call(s32[13]{0:T(128)} %concatenate.12.info, bf16[2,256,2048]{2,1,0:T(8,128)(2,1)} %refs_1_.7, bf16[2,256,2048]{2,1,0:T(8,128)(2,1)} %refs_1_.7, bf16[2,256,2048]{2,1,0:T(8,128)(2,1)} %copy-done, ...), custom_call_target="tpu_custom_call" | custom-call | bytes 21600000 | tf_op jit(solution)/shard_map/conv/pallas_call | solution.py:355
  27.9 3.4 %collective-permute-start.13 = (bf16[64,2048]{1,0:T(8,128)(2,1)S(1)}, bf16[64,2048]{1,0:T(8,128)(2,1)S(1)}, u32[]{:S(2)}, u32[]{:S(2)}) collective-permute-start(bf16[64,2048]{1,0:T(8,128)(2,1)S(1)} %collective-permute-done.10.refs_23_), channel_id=1, source_target_pairs={{0,4},{4,8},{8,12},{12,14},{14,10},{10,6},{6,2},{2,0},{1,5},{5,9},... | collective-permute-start | bytes 786440 | tf_op jit(solution)/shard_map/ppermute | solution.py:758
  31.2 2.0 %collective-permute-start.4 = (bf16[128,2048]{1,0:T(8,128)(2,1)}, bf16[128,2048]{1,0:T(8,128)(2,1)S(1)}, u32[]{:S(2)}, u32[]{:S(2)}) collective-permute-start(bf16[128,2048]{1,0:T(8,128)(2,1)} %get-tuple-element.59), channel_id=1, source_target_pairs={{0,4},{4,8},{8,12},{12,14},{14,10},{10,6},{6,2},{2,0},{1,5},{5,9},... | collective-permute-start | bytes 1572872 | tf_op jit(solution)/shard_map/ppermute | solution.py:779
  33.2 7.4 %conv.5 = (f32[2,544,256]{2,1,0:T(8,128)}, bf16[2,640,256]{2,1,0:T(8,128)(2,1)}, f32[128,2048]{1,0:T(8,128)}, f32[128,2048]{1,0:T(8,128)}) custom-call(s32[13]{0:T(128)} %concatenate.12.info, bf16[2,256,2048]{2,1,0:T(8,128)(2,1)} %refs_1_.7, bf16[2,256,2048]{2,1,0:T(8,128)(2,1)} %refs_1_.7, bf16[2,256,2048]{2,1,0:T(8,128)(2,1)} %copy-done, ...), custom_call_target="tpu_custom_call" | custom-call | bytes 21600000 | tf_op jit(solution)/shard_map/conv/pallas_call | solution.py:355
  40.7 2.1 %collective-permute-start.16 = (bf16[64,2048]{1,0:T(8,128)(2,1)S(1)}, bf16[64,2048]{1,0:T(8,128)(2,1)S(1)}, u32[]{:S(2)}, u32[]{:S(2)}) collective-permute-start(bf16[64,2048]{1,0:T(8,128)(2,1)S(1)} %collective-permute-done.13.refs_21_), channel_id=1, source_target_pairs={{0,4},{4,8},{8,12},{12,14},{14,10},{10,6},{6,2},{2,0},{1,5},{5,9},... | collective-permute-start | bytes 786440 | tf_op jit(solution)/shard_map/ppermute | solution.py:758
  42.8 1.6 %collective-permute-start.11 = (bf16[128,2048]{1,0:T(8,128)(2,1)S(1)}, bf16[128,2048]{1,0:T(8,128)(2,1)S(1)}, u32[]{:S(2)}, u32[]{:S(2)}) collective-permute-start(bf16[128,2048]{1,0:T(8,128)(2,1)S(1)} %pad_maximum_fusion.1), channel_id=1, source_target_pairs={{0,16},{1,17},{2,18},{3,19},{4,20},{5,21},{6,22},{7,23},{8,24},{9,... | collective-permute-start | bytes 1572872 | tf_op jit(solution)/shard_map/ppermute | solution.py:821
  44.4 7.5 %conv.6 = (f32[2,544,256]{2,1,0:T(8,128)}, bf16[2,640,256]{2,1,0:T(8,128)(2,1)}, f32[128,2048]{1,0:T(8,128)}, f32[128,2048]{1,0:T(8,128)}) custom-call(s32[13]{0:T(128)} %concatenate.12.info, bf16[2,256,2048]{2,1,0:T(8,128)(2,1)} %refs_1_.7, bf16[2,256,2048]{2,1,0:T(8,128)(2,1)} %refs_1_.7, bf16[2,256,2048]{2,1,0:T(8,128)(2,1)} %copy-done, ...), custom_call_target="tpu_custom_call" | custom-call | bytes 21600000 | tf_op jit(solution)/shard_map/conv/pallas_call | solution.py:355
  52.0 2.0 %collective-permute-done.16.refs_24_ = bf16[64,2048]{1,0:T(8,128)(2,1)S(1)} collective-permute-done((bf16[64,2048]{1,0:T(8,128)(2,1)S(1)}, bf16[64,2048]{1,0:T(8,128)(2,1)S(1)}, u32[]{:S(2)}, u32[]{:S(2)}) %collective-permute-start.16) | collective-permute-done | bytes 262176 | tf_op jit(solution)/shard_map/ppermute | solution.py:758
  54.0 1.5 %collective-permute-start.14 = (bf16[128,2048]{1,0:T(8,128)(2,1)S(1)}, bf16[128,2048]{1,0:T(8,128)(2,1)S(1)}, u32[]{:S(2)}, u32[]{:S(2)}) collective-permute-start(bf16[128,2048]{1,0:T(8,128)(2,1)S(1)} %pad_maximum_fusion.2), channel_id=1, source_target_pairs={{0,16},{1,17},{2,18},{3,19},{4,20},{5,21},{6,22},{7,23},{8,24},{9,... | collective-permute-start | bytes 1572872 | tf_op jit(solution)/shard_map/ppermute | solution.py:821
  55.8 1.7 %collective-permute-start.17 = (bf16[64,2048]{1,0:T(8,128)(2,1)S(1)}, bf16[64,2048]{1,0:T(8,128)(2,1)S(1)}, u32[]{:S(2)}, u32[]{:S(2)}) collective-permute-start(bf16[64,2048]{1,0:T(8,128)(2,1)S(1)} %collective-permute-done.16.refs_24_), channel_id=1, source_target_pairs={{0,4},{4,8},{8,12},{12,14},{14,10},{10,6},{6,2},{2,0},{1,5},{5,9},... | collective-permute-start | bytes 786440 | tf_op jit(solution)/shard_map/ppermute | solution.py:758
  60.0 5.2 %collective-permute-done.17.refs_25_ = bf16[64,2048]{1,0:T(8,128)(2,1)S(1)} collective-permute-done((bf16[64,2048]{1,0:T(8,128)(2,1)S(1)}, bf16[64,2048]{1,0:T(8,128)(2,1)S(1)}, u32[]{:S(2)}, u32[]{:S(2)}) %collective-permute-start.17) | collective-permute-done | bytes 262176 | tf_op jit(solution)/shard_map/ppermute | solution.py:758
  65.1 7.4 %conv.7 = (f32[2,544,256]{2,1,0:T(8,128)}, bf16[2,640,256]{2,1,0:T(8,128)(2,1)}, f32[128,2048]{1,0:T(8,128)}, f32[128,2048]{1,0:T(8,128)}) custom-call(s32[13]{0:T(128)} %concatenate.12.info, bf16[2,256,2048]{2,1,0:T(8,128)(2,1)} %refs_1_.7, bf16[2,256,2048]{2,1,0:T(8,128)(2,1)} %refs_1_.7, bf16[2,256,2048]{2,1,0:T(8,128)(2,1)} %copy-done, ...), custom_call_target="tpu_custom_call" | custom-call | bytes 21600000 | tf_op jit(solution)/shard_map/conv/pallas_call | solution.py:355
  75.0 12.3 %back.2 = (bf16[2,2,256,256]{3,2,1,0:T(8,128)(2,1)}, bf16[2,2,256,256]{3,2,1,0:T(8,128)(2,1)}, f32[2,40,256]{2,1,0:T(8,128)}) custom-call(s32[13]{0:T(128)} %concatenate.12.info, bf16[2,256,2048]{2,1,0:T(8,128)(2,1)} %refs_0_.11, bf16[2,256,2048]{2,1,0:T(8,128)(2,1)} %collective-permute-done.3.refs_18_.refs_1_, bf16[2,64,1024]{2,1,0:T(8,128)(2,1)} %copy-done.1, ...), custom_call_target="tpu_custom_call" | custom-call | bytes 43200000 | tf_op jit(solution)/shard_map/back/pallas_call | solution.py:601
  88.7 1.5 %collective-permute-start.22 = (bf16[128,2048]{1,0:T(8,128)(2,1)S(1)}, bf16[128,2048]{1,0:T(8,128)(2,1)S(1)}, u32[]{:S(2)}, u32[]{:S(2)}) collective-permute-start(bf16[128,2048]{1,0:T(8,128)(2,1)S(1)} %add_convert_fusion.1), channel_id=1, source_target_pairs={{4,0},{8,4},{12,8},{14,12},{10,14},{6,10},{2,6},{0,2},{5,1},{9,5},... | collective-permute-start | bytes 1572872 | tf_op jit(solution)/shard_map/ppermute | solution.py:779
  90.2 2.4 %collective-permute-done.18.refs_22_ = bf16[192,2048]{1,0:T(8,128)(2,1)S(1)} collective-permute-done((bf16[192,2048]{1,0:T(8,128)(2,1)S(1)}, bf16[192,2048]{1,0:T(8,128)(2,1)S(1)}, u32[]{:S(2)}, u32[]{:S(2)}) %collective-permute-start.18) | collective-permute-done | bytes 786464 | tf_op jit(solution)/shard_map/ppermute | solution.py:821
  93.5 12.7 %back.3 = (bf16[2,2,256,256]{3,2,1,0:T(8,128)(2,1)}, bf16[2,2,256,256]{3,2,1,0:T(8,128)(2,1)}, f32[8,40,128]{2,1,0:T(8,128)}) custom-call(s32[13]{0:T(128)} %concatenate.12.info, bf16[2,256,2048]{2,1,0:T(8,128)(2,1)} %refs_0_.11, bf16[2,256,2048]{2,1,0:T(8,128)(2,1)} %collective-permute-done.3.refs_18_.refs_1_, bf16[2,64,1024]{2,1,0:T(8,128)(2,1)} %copy-done.1, ...), custom_call_target="tpu_custom_call" | custom-call | bytes 43200000 | tf_op jit(solution)/shard_map/back/pallas_call | solution.py:601
  107.3 1.6 %collective-permute-start.23 = (bf16[128,2048]{1,0:T(8,128)(2,1)}, bf16[128,2048]{1,0:T(8,128)(2,1)S(1)}, u32[]{:S(2)}, u32[]{:S(2)}) collective-permute-start(bf16[128,2048]{1,0:T(8,128)(2,1)} %add_convert_fusion), channel_id=1, source_target_pairs={{0,4},{4,8},{8,12},{12,14},{14,10},{10,6},{6,2},{2,0},{1,5},{5,9},... | collective-permute-start | bytes 1572872 | tf_op jit(solution)/shard_map/ppermute | solution.py:854
  108.9 4.9 %all-to-all-start = ((f32[8,40,128]{2,1,0:T(8,128)}), f32[8,40,128]{2,1,0:T(8,128)S(1)}, u32[]{:S(2)}, u32[]{:S(2)}) async-start(f32[8,40,128]{2,1,0:T(8,128)} %get-tuple-element.91), calls=%async_computation | async-start | bytes 327680 | tf_op jit(solution)/shard_map/all_to_all | solution.py:851
  115.5 4.1 %place.1 = bf16[2,256,2048]{2,1,0:T(8,128)(2,1)} custom-call(s32[13]{0:T(128)} %concatenate.12.info, bf16[2,2,256,256]{3,2,1,0:T(8,128)(2,1)} %get-tuple-element.79.refs_0_, bf16[2,2,256,256]{3,2,1,0:T(8,128)(2,1)} %copy-done.22, bf16[2,2,256,256]{3,2,1,0:T(8,128)(2,1)} %get-tuple-element.94.refs_2_, bf16[2,2,256,256]{3,2,1,0:T(8,128)(2,1)} %copy-done.23), custom_call_target="tpu_custom_call" | custom-call | bytes 10800000 | tf_op jit(solution)/shard_map/place/pallas_call | solution.py:666
  119.6 8.1 %all-to-all-done = f32[8,40,128]{2,1,0:T(8,128)S(1)} async-done(((f32[8,40,128]{2,1,0:T(8,128)}), f32[8,40,128]{2,1,0:T(8,128)S(1)}, u32[]{:S(2)}, u32[]{:S(2)}) %all-to-all-start) | async-done | bytes 163872 | tf_op jit(solution)/shard_map/all_to_all | solution.py:851
  (107 shorter events, 18.4 us)
Async XLA Ops:
  0.7 18.7 %collective-permute-start.2 = (bf16[2,256,2048]{2,1,0:T(8,128)(2,1)}, bf16[2,256,2048]{2,1,0:T(8,128)(2,1)S(1)}, u32[]{:S(2)}, u32[]{:S(2)}) collective-permute-start(bf16[2,256,2048]{2,1,0:T(8,128)(2,1)} %refs_1_.7), channel_id=1, source_target_pairs={{0,1},{1,0},{2,3},{3,2},{4,5},{5,4},{6,7},{7,6},{8,9},{9,8},{10,11... | collective-permute-start | bytes 6291464 | tf_op jit(solution)/shard_map/ppermute | solution.py:746
  1.2 18.2 %collective-permute-start.3 = (bf16[2,256,2048]{2,1,0:T(8,128)(2,1)}, bf16[2,256,2048]{2,1,0:T(8,128)(2,1)}, u32[]{:S(2)}, u32[]{:S(2)}) collective-permute-start(bf16[2,256,2048]{2,1,0:T(8,128)(2,1)} %refs_0_.11), channel_id=1, source_target_pairs={{0,1},{1,0},{2,3},{3,2},{4,5},{5,4},{6,7},{7,6},{8,9},{9,8},{10,11... | collective-permute-start | bytes 6291464 | tf_op jit(solution)/shard_map/ppermute | solution.py:747
  3.2 16.2 %collective-permute-start = (bf16[2,64,1024]{2,1,0:T(8,128)(2,1)}, bf16[2,64,1024]{2,1,0:T(8,128)(2,1)S(1)}, u32[]{:S(2)}, u32[]{:S(2)}) collective-permute-start(bf16[2,64,1024]{2,1,0:T(8,128)(2,1)} %get-tuple-element.53), channel_id=1, source_target_pairs={{1,2},{2,1},{3,4},{4,3},{5,6},{6,5},{7,8},{8,7},{9,10},{10,9},{11,... | collective-permute-start | bytes 786440 | tf_op jit(solution)/shard_map/ppermute | solution.py:744
  3.9 10.1 %collective-permute-start.1 = (bf16[2,32,1024]{2,1,0:T(8,128)(2,1)}, bf16[2,32,1024]{2,1,0:T(8,128)(2,1)S(1)}, u32[]{:S(2)}, u32[]{:S(2)}) collective-permute-start(bf16[2,32,1024]{2,1,0:T(8,128)(2,1)} %get-tuple-element.54), channel_id=1, source_target_pairs={{1,3},{2,0},{3,5},{4,2},{5,7},{6,4},{7,9},{8,6},{9,11},{10,8},{11,... | collective-permute-start | bytes 393224 | tf_op jit(solution)/shard_map/ppermute | solution.py:745
  5.2 22.6 %collective-permute-start.10 = (bf16[64,2048]{1,0:T(8,128)(2,1)S(1)}, bf16[64,2048]{1,0:T(8,128)(2,1)S(1)}, u32[]{:S(2)}, u32[]{:S(2)}) collective-permute-start(bf16[64,2048]{1,0:T(8,128)(2,1)S(1)} %constant_dynamic-slice_fusion), channel_id=1, source_target_pairs={{0,4},{4,8},{8,12},{12,14},{14,10},{10,6},{6,2},{2,0},{1,5},{5,9},... | collective-permute-start | bytes 786440 | tf_op jit(solution)/shard_map/ppermute | solution.py:758
  14.0 13.9 %collective-permute-start.9 = (bf16[64,2048]{1,0:T(8,128)(2,1)S(1)}, bf16[64,2048]{1,0:T(8,128)(2,1)S(1)}, u32[]{:S(2)}, u32[]{:S(2)}) collective-permute-start(bf16[64,2048]{1,0:T(8,128)(2,1)S(1)} %constant_dynamic-slice_fusion), channel_id=1, source_target_pairs={{4,0},{8,4},{12,8},{14,12},{10,14},{6,10},{2,6},{0,2},{5,1},{9,5},... | collective-permute-start | bytes 786440 | tf_op jit(solution)/shard_map/ppermute | solution.py:761
  27.9 12.8 %collective-permute-start.13 = (bf16[64,2048]{1,0:T(8,128)(2,1)S(1)}, bf16[64,2048]{1,0:T(8,128)(2,1)S(1)}, u32[]{:S(2)}, u32[]{:S(2)}) collective-permute-start(bf16[64,2048]{1,0:T(8,128)(2,1)S(1)} %collective-permute-done.10.refs_23_), channel_id=1, source_target_pairs={{0,4},{4,8},{8,12},{12,14},{14,10},{10,6},{6,2},{2,0},{1,5},{5,9},... | collective-permute-start | bytes 786440 | tf_op jit(solution)/shard_map/ppermute | solution.py:758
  31.2 9.4 %collective-permute-start.12 = (bf16[64,2048]{1,0:T(8,128)(2,1)S(1)}, bf16[64,2048]{1,0:T(8,128)(2,1)S(1)}, u32[]{:S(2)}, u32[]{:S(2)}) collective-permute-start(bf16[64,2048]{1,0:T(8,128)(2,1)S(1)} %collective-permute-done.9.refs_22_), channel_id=1, source_target_pairs={{4,0},{8,4},{12,8},{14,12},{10,14},{6,10},{2,6},{0,2},{5,1},{9,5},... | collective-permute-start | bytes 786440 | tf_op jit(solution)/shard_map/ppermute | solution.py:761
  31.2 26.4 %collective-permute-start.4 = (bf16[128,2048]{1,0:T(8,128)(2,1)}, bf16[128,2048]{1,0:T(8,128)(2,1)S(1)}, u32[]{:S(2)}, u32[]{:S(2)}) collective-permute-start(bf16[128,2048]{1,0:T(8,128)(2,1)} %get-tuple-element.59), channel_id=1, source_target_pairs={{0,4},{4,8},{8,12},{12,14},{14,10},{10,6},{6,2},{2,0},{1,5},{5,9},... | collective-permute-start | bytes 1572872 | tf_op jit(solution)/shard_map/ppermute | solution.py:779
  33.2 24.3 %collective-permute-start.5 = (bf16[128,2048]{1,0:T(8,128)(2,1)}, bf16[128,2048]{1,0:T(8,128)(2,1)S(1)}, u32[]{:S(2)}, u32[]{:S(2)}) collective-permute-start(bf16[128,2048]{1,0:T(8,128)(2,1)} %get-tuple-element.65), channel_id=1, source_target_pairs={{4,0},{8,4},{12,8},{14,12},{10,14},{6,10},{2,6},{0,2},{5,1},{9,5},... | collective-permute-start | bytes 1572872 | tf_op jit(solution)/shard_map/ppermute | solution.py:779
  40.7 13.3 %collective-permute-start.16 = (bf16[64,2048]{1,0:T(8,128)(2,1)S(1)}, bf16[64,2048]{1,0:T(8,128)(2,1)S(1)}, u32[]{:S(2)}, u32[]{:S(2)}) collective-permute-start(bf16[64,2048]{1,0:T(8,128)(2,1)S(1)} %collective-permute-done.13.refs_21_), channel_id=1, source_target_pairs={{0,4},{4,8},{8,12},{12,14},{14,10},{10,6},{6,2},{2,0},{1,5},{5,9},... | collective-permute-start | bytes 786440 | tf_op jit(solution)/shard_map/ppermute | solution.py:758
  42.7 13.1 %collective-permute-start.15 = (bf16[64,2048]{1,0:T(8,128)(2,1)S(1)}, bf16[64,2048]{1,0:T(8,128)(2,1)S(1)}, u32[]{:S(2)}, u32[]{:S(2)}) collective-permute-start(bf16[64,2048]{1,0:T(8,128)(2,1)S(1)} %collective-permute-done.12.refs_25_), channel_id=1, source_target_pairs={{4,0},{8,4},{12,8},{14,12},{10,14},{6,10},{2,6},{0,2},{5,1},{9,5},... | collective-permute-start | bytes 786440 | tf_op jit(solution)/shard_map/ppermute | solution.py:761
  42.8 29.9 %collective-permute-start.11 = (bf16[128,2048]{1,0:T(8,128)(2,1)S(1)}, bf16[128,2048]{1,0:T(8,128)(2,1)S(1)}, u32[]{:S(2)}, u32[]{:S(2)}) collective-permute-start(bf16[128,2048]{1,0:T(8,128)(2,1)S(1)} %pad_maximum_fusion.1), channel_id=1, source_target_pairs={{0,16},{1,17},{2,18},{3,19},{4,20},{5,21},{6,22},{7,23},{8,24},{9,... | collective-permute-start | bytes 1572872 | tf_op jit(solution)/shard_map/ppermute | solution.py:821
  54.0 20.1 %collective-permute-start.14 = (bf16[128,2048]{1,0:T(8,128)(2,1)S(1)}, bf16[128,2048]{1,0:T(8,128)(2,1)S(1)}, u32[]{:S(2)}, u32[]{:S(2)}) collective-permute-start(bf16[128,2048]{1,0:T(8,128)(2,1)S(1)} %pad_maximum_fusion.2), channel_id=1, source_target_pairs={{0,16},{1,17},{2,18},{3,19},{4,20},{5,21},{6,22},{7,23},{8,24},{9,... | collective-permute-start | bytes 1572872 | tf_op jit(solution)/shard_map/ppermute | solution.py:821
  55.8 9.3 %collective-permute-start.17 = (bf16[64,2048]{1,0:T(8,128)(2,1)S(1)}, bf16[64,2048]{1,0:T(8,128)(2,1)S(1)}, u32[]{:S(2)}, u32[]{:S(2)}) collective-permute-start(bf16[64,2048]{1,0:T(8,128)(2,1)S(1)} %collective-permute-done.16.refs_24_), channel_id=1, source_target_pairs={{0,4},{4,8},{8,12},{12,14},{14,10},{10,6},{6,2},{2,0},{1,5},{5,9},... | collective-permute-start | bytes 786440 | tf_op jit(solution)/shard_map/ppermute | solution.py:758
  57.7 29.7 %collective-permute-start.6 = (bf16[128,2048]{1,0:T(8,128)(2,1)S(1)}, bf16[128,2048]{1,0:T(8,128)(2,1)S(1)}, u32[]{:S(2)}, u32[]{:S(2)}) collective-permute-start(bf16[128,2048]{1,0:T(8,128)(2,1)S(1)} %add_convert_fusion.4), channel_id=1, source_target_pairs={{0,4},{4,8},{8,12},{12,14},{14,10},{10,6},{6,2},{2,0},{1,5},{5,9},... | collective-permute-start | bytes 1572872 | tf_op jit(solution)/shard_map/ppermute | solution.py:779
  58.8 28.6 %collective-permute-start.7 = (bf16[128,2048]{1,0:T(8,128)(2,1)S(1)}, bf16[128,2048]{1,0:T(8,128)(2,1)S(1)}, u32[]{:S(2)}, u32[]{:S(2)}) collective-permute-start(bf16[128,2048]{1,0:T(8,128)(2,1)S(1)} %add_convert_fusion.3), channel_id=1, source_target_pairs={{4,0},{8,4},{12,8},{14,12},{10,14},{6,10},{2,6},{0,2},{5,1},{9,5},... | collective-permute-start | bytes 1572872 | tf_op jit(solution)/shard_map/ppermute | solution.py:779
  65.1 9.0 %collective-permute-start.8 = (bf16[2,64,1024]{2,1,0:T(8,128)(2,1)S(1)}, bf16[2,64,1024]{2,1,0:T(8,128)(2,1)S(1)}, u32[]{:S(2)}, u32[]{:S(2)}) collective-permute-start(bf16[2,64,1024]{2,1,0:T(8,128)(2,1)S(1)} %copy-done.2), channel_id=1, source_target_pairs={{0,1},{1,0},{2,3},{3,2},{4,5},{5,4},{6,7},{7,6},{8,9},{9,8},{10,11... | collective-permute-start | bytes 786440 | tf_op jit(solution)/shard_map/ppermute | solution.py:793
  72.7 20.0 %collective-permute-start.18 = (bf16[192,2048]{1,0:T(8,128)(2,1)S(1)}, bf16[192,2048]{1,0:T(8,128)(2,1)S(1)}, u32[]{:S(2)}, u32[]{:S(2)}) collective-permute-start(bf16[192,2048]{1,0:T(8,128)(2,1)S(1)} %pad_maximum_fusion), channel_id=1, source_target_pairs={{0,16},{1,17},{2,18},{3,19},{4,20},{5,21},{6,22},{7,23},{8,24},{9,... | collective-permute-start | bytes 2359304 | tf_op jit(solution)/shard_map/ppermute | solution.py:821
  87.5 18.8 %collective-permute-start.21 = (bf16[128,2048]{1,0:T(8,128)(2,1)S(1)}, bf16[128,2048]{1,0:T(8,128)(2,1)S(1)}, u32[]{:S(2)}, u32[]{:S(2)}) collective-permute-start(bf16[128,2048]{1,0:T(8,128)(2,1)S(1)} %add_convert_fusion.2), channel_id=1, source_target_pairs={{0,4},{4,8},{8,12},{12,14},{14,10},{10,6},{6,2},{2,0},{1,5},{5,9},... | collective-permute-start | bytes 1572872 | tf_op jit(solution)/shard_map/ppermute | solution.py:779
  88.7 17.6 %collective-permute-start.22 = (bf16[128,2048]{1,0:T(8,128)(2,1)S(1)}, bf16[128,2048]{1,0:T(8,128)(2,1)S(1)}, u32[]{:S(2)}, u32[]{:S(2)}) collective-permute-start(bf16[128,2048]{1,0:T(8,128)(2,1)S(1)} %add_convert_fusion.1), channel_id=1, source_target_pairs={{4,0},{8,4},{12,8},{14,12},{10,14},{6,10},{2,6},{0,2},{5,1},{9,5},... | collective-permute-start | bytes 1572872 | tf_op jit(solution)/shard_map/ppermute | solution.py:779
  90.2 23.6 %collective-permute-start.19 = (bf16[2,2,256,256]{3,2,1,0:T(8,128)(2,1)}, bf16[2,2,256,256]{3,2,1,0:T(8,128)(2,1)S(1)}, u32[]{:S(2)}, u32[]{:S(2)}) collective-permute-start(bf16[2,2,256,256]{3,2,1,0:T(8,128)(2,1)} %get-tuple-element.93), channel_id=1, source_target_pairs={{0,1},{1,0},{2,3},{3,2},{4,5},{5,4},{6,7},{7,6},{8,9},{9,8},{10,11... | collective-permute-start | bytes 1572872 | tf_op jit(solution)/shard_map/ppermute | solution.py:849
  107.3 21.7 %collective-permute-start.23 = (bf16[128,2048]{1,0:T(8,128)(2,1)}, bf16[128,2048]{1,0:T(8,128)(2,1)S(1)}, u32[]{:S(2)}, u32[]{:S(2)}) collective-permute-start(bf16[128,2048]{1,0:T(8,128)(2,1)} %add_convert_fusion), channel_id=1, source_target_pairs={{0,4},{4,8},{8,12},{12,14},{14,10},{10,6},{6,2},{2,0},{1,5},{5,9},... | collective-permute-start | bytes 1572872 | tf_op jit(solution)/shard_map/ppermute | solution.py:854
  108.9 18.8 %all-to-all-start = ((f32[8,40,128]{2,1,0:T(8,128)}), f32[8,40,128]{2,1,0:T(8,128)S(1)}, u32[]{:S(2)}, u32[]{:S(2)}) async-start(f32[8,40,128]{2,1,0:T(8,128)} %get-tuple-element.91), calls=%async_computation | async-start | bytes 327680 | tf_op jit(solution)/shard_map/all_to_all | solution.py:851
  (28 other events, 241.5 us)
